TPU v7x, 32 devices: a whole 2x2x4 slice. The times are simulated.
32 devices in a mesh: seq: 16 (over z, x, core), head: 2 (over y).
Axes of the slice: x: 2, y: 2, z: 4, core: 2. Of those that a mesh axis runs over, the one named last changes fastest.
Arguments:
- query: bfloat16 [2048, 8192], P(('seq', 'head')), may hold values from -6 to 6
- key: bfloat16 [2048, 8192], P(('seq', 'head')), may hold values from -6 to 6
- value: bfloat16 [2048, 8192], P(('seq', 'head')), may hold values from -6 to 6
- cotangent: bfloat16 [2048, 8192], P(('seq', 'head')), may hold values from -6 to 6
- gain: float32 [8192], P('head'), may hold values from 0.5 to 1.5
- incoming_state: float32 [64, 128, 128], P('head'), may hold values from -288 to 288
Outputs:
- output: bfloat16 [2048, 8192], P(('seq', 'head'))
- grad_query: bfloat16 [2048, 8192], P(('seq', 'head'))
- grad_key: bfloat16 [2048, 8192], P(('seq', 'head'))
- grad_value: bfloat16 [2048, 8192], P(('seq', 'head'))
All inputs are finite; a program needn't handle non-finite values.
Results may differ from a plain program's by a relative error of at most 0.0058.
Values may be sent and summed in bfloat16 or wider, within the bound.
A program may use at most 128 MiB of HBM per device.

v0:
```python
import functools

import jax
import jax.numpy as jnp
from jax import lax
from jax.experimental import pallas as pl
from jax.experimental.pallas import tpu as pltpu
from jax.sharding import PartitionSpec as P

HEAD_DIM = 128
EPSILON = 1e-06
MESH = pl.DeviceIdType.MESH
F32 = jnp.float32
BF16 = jnp.bfloat16

NT = (((1,), (1,)), ((), ()))
TN = (((0,), (0,)), ((), ()))
NN = (((1,), (0,)), ((), ()))


def dot(a, b, dims):
    return lax.dot_general(a, b, dims, preferred_element_type=F32)


def kernel(plan, q_hbm, k_hbm, v_hbm, y_hbm, gain_hbm, s0_hbm, o_hbm, gq_hbm, gk_hbm, gv_hbm,
           xin, xout, part, cum, gcum, pin, psend, sin, ssend, tot, gain,
           in_send, in_recv, out_send, out_recv, p_send, p_recv, s_send, s_recv, gain_sem):
    n_groups, sub, n_head, rows, heads, step = plan
    peers = sub * n_head
    chunks = heads // step
    block = rows * n_head
    width = heads * HEAD_DIM
    span = step * HEAD_DIM
    seq, hd = lax.axis_index("seq"), lax.axis_index("head")
    group, j = seq // sub, lax.rem(seq, sub)
    me = j * n_head + hd

    def place(p):
        other = lax.rem(me + p, peers)
        return other, (group * sub + other // n_head, lax.rem(other, n_head))

    def column(other, c):
        owner = lax.rem(other, n_head) * (sub * heads) + (other // n_head) * heads + c * step
        return pl.ds(pl.multiple_of(owner * HEAD_DIM, span), span)

    def strip(index):
        return pl.ds(pl.multiple_of(index * rows, rows), rows)

    later = (seq + sub, hd)
    earlier = (seq - sub, hd)
    barrier = pltpu.get_barrier_semaphore()

    def greet(p, carry):
        _, device = place(p)
        pl.semaphore_signal(barrier, inc=1, device_id=device, device_id_type=MESH)
        return carry

    lax.fori_loop(1, peers, greet, 0)

    @pl.when(group > 0)
    def _():
        pl.semaphore_signal(barrier, inc=1, device_id=earlier, device_id_type=MESH)

    @pl.when(group < n_groups - 1)
    def _():
        pl.semaphore_signal(barrier, inc=1, device_id=later, device_id_type=MESH)

    sources = ((k_hbm, v_hbm), (q_hbm, y_hbm))
    targets = ((o_hbm, gq_hbm), (gk_hbm, gv_hbm))

    for phase in range(2):
        for c in range(chunks):
            cols = pl.ds(c * span, span)
            for a in range(2):
                pltpu.make_async_copy(
                    sources[phase][a].at[:, column(me, c)],
                    xin.at[2 * phase + a, strip(me), cols],
                    in_recv.at[phase, c],
                ).start()

    gains = pltpu.make_async_copy(gain_hbm, gain, gain_sem)
    gains.start()

    @pl.when(group == 0)
    def _():
        for c in range(chunks):
            pltpu.make_async_copy(
                s0_hbm.at[pl.ds(j * heads + c * step, step)],
                pin.at[pl.ds(c * step, step)],
                p_recv.at[c],
            ).start()

    if n_groups == 1:
        pl.semaphore_wait(barrier, peers - 1)
    else:
        inner = jnp.logical_and(group > 0, group < n_groups - 1)

        @pl.when(inner)
        def _():
            pl.semaphore_wait(barrier, peers + 1)

        @pl.when(jnp.logical_not(inner))
        def _():
            pl.semaphore_wait(barrier, peers)

    for phase in range(2):
        for c in range(chunks):
            cols = pl.ds(c * span, span)

            def scatter(p, carry, phase=phase, c=c, cols=cols):
                other, device = place(p)
                for a in range(2):
                    pltpu.make_async_remote_copy(
                        src_ref=sources[phase][a].at[:, column(other, c)],
                        dst_ref=xin.at[2 * phase + a, strip(me), cols],
                        send_sem=in_send.at[phase, c],
                        recv_sem=in_recv.at[phase, c],
                        device_id=device,
                        device_id_type=MESH,
                    ).start()
                return carry

            lax.fori_loop(1, peers, scatter, 0)

    def arrived(phase, c):
        ref = xin.at[pl.ds(2 * phase, 2), :, pl.ds(c * span, span)]
        pltpu.make_async_copy(ref, ref, in_recv.at[phase, c]).wait()

    def give(phase, c):
        cols = pl.ds(c * span, span)

        def back(p, carry):
            other, device = place(p)
            for a in range(2):
                pltpu.make_async_remote_copy(
                    src_ref=xout.at[2 * phase + a, strip(other), cols],
                    dst_ref=targets[phase][a].at[:, column(me, c)],
                    send_sem=out_send.at[phase, c],
                    recv_sem=out_recv.at[phase, c],
                    device_id=device,
                    device_id_type=MESH,
                ).start()
            return carry

        lax.fori_loop(1, peers, back, 0)
        for a in range(2):
            pltpu.make_async_copy(
                xout.at[2 * phase + a, strip(me), cols],
                targets[phase][a].at[:, column(me, c)],
                out_recv.at[phase, c],
            ).start()

    def state_copy(src, dst, send, recv, c, device):
        piece = pl.ds(c * step, step)
        return pltpu.make_async_remote_copy(
            src_ref=src.at[piece], dst_ref=dst.at[piece], send_sem=send.at[c],
            recv_sem=recv.at[c], device_id=device, device_id_type=MESH)

    def pass_prefix(c):
        piece = pl.ds(c * step, step)
        pltpu.make_async_copy(pin.at[piece], pin.at[piece], p_recv.at[c]).wait()

        @pl.when(group < n_groups - 1)
        def _():
            psend[c * step:(c + 1) * step] = (
                pin[c * step:(c + 1) * step] + tot[c * step:(c + 1) * step])
            state_copy(psend, pin, p_send, p_recv, c, later).start()

    for c in range(chunks):
        arrived(0, c)
        for h in range(c * step, (c + 1) * step):
            hc = slice(h * HEAD_DIM, (h + 1) * HEAD_DIM)
            run = jnp.zeros((HEAD_DIM, HEAD_DIM), F32)
            for b in range(sub):
                r = slice(b * block, (b + 1) * block)
                cum[h, b] = run
                run = run + dot(xin[0, r, hc], xin[1, r, hc], TN)
            tot[h] = run

        @pl.when(group == 0)
        def _(c=c):
            pass_prefix(c)

    row = lax.broadcasted_iota(jnp.int32, (block, block), 0)
    col = lax.broadcasted_iota(jnp.int32, (block, block), 1)
    causal = col <= row
    gains.wait()

    for c in range(chunks):
        @pl.when(group > 0)
        def _(c=c):
            pass_prefix(c)

    for c in range(chunks):
        arrived(1, c)
        for h in range(c * step, (c + 1) * step):
            hc = slice(h * HEAD_DIM, (h + 1) * HEAD_DIM)
            g = gain[pl.ds(j * heads + h, 1), :]
            carried = pin[h]
            run = jnp.zeros((HEAD_DIM, HEAD_DIM), F32)
            for b in reversed(range(sub)):
                r = slice(b * block, (b + 1) * block)
                k, v, q, up = xin[0, r, hc], xin[1, r, hc], xin[2, r, hc], xin[3, r, hc]
                state = (carried + cum[h, b]).astype(BF16)
                w = jnp.where(causal, dot(q, k, NT), 0.0).astype(BF16)
                att = dot(w, v, NN) + dot(q, state, NN)
                inv = lax.rsqrt(jnp.mean(att * att, axis=-1, keepdims=True) + EPSILON)
                normed = att * inv
                xout[0, r, hc] = (normed * g).astype(BF16)
                scaled = up.astype(F32) * g
                ga = ((scaled - normed * jnp.mean(scaled * normed, axis=-1, keepdims=True))
                      * inv).astype(BF16)
                gw = jnp.where(causal, dot(ga, v, NT), 0.0).astype(BF16)
                xout[1, r, hc] = (dot(gw, k, NN) + dot(ga, state, NT)).astype(BF16)
                part[0, r, hc] = dot(gw, q, TN)
                part[1, r, hc] = dot(w, ga, TN)
                gcum[h, b] = run
                run = run + dot(q, ga, TN)
            tot[h] = run

        @pl.when(jnp.logical_and(group == n_groups - 1, group > 0))
        def _(c=c):
            ssend[c * step:(c + 1) * step] = tot[c * step:(c + 1) * step]
            state_copy(ssend, sin, s_send, s_recv, c, earlier).start()

        give(0, c)

    for c in range(chunks):
        piece = pl.ds(c * step, step)

        @pl.when(group == n_groups - 1)
        def _(c=c):
            sin[c * step:(c + 1) * step] = jnp.zeros((step, HEAD_DIM, HEAD_DIM), F32)

        @pl.when(group < n_groups - 1)
        def _(c=c, piece=piece):
            pltpu.make_async_copy(sin.at[piece], sin.at[piece], s_recv.at[c]).wait()

            @pl.when(group > 0)
            def _():
                ssend[c * step:(c + 1) * step] = (
                    sin[c * step:(c + 1) * step] + tot[c * step:(c + 1) * step])
                state_copy(ssend, sin, s_send, s_recv, c, earlier).start()

        for h in range(c * step, (c + 1) * step):
            hc = slice(h * HEAD_DIM, (h + 1) * HEAD_DIM)
            after = sin[h]
            for b in range(sub):
                r = slice(b * block, (b + 1) * block)
                suffix = (after + gcum[h, b]).astype(BF16)
                xout[2, r, hc] = (part[0, r, hc] + dot(xin[1, r, hc], suffix, NT)).astype(BF16)
                xout[3, r, hc] = (part[1, r, hc] + dot(xin[0, r, hc], suffix, NN)).astype(BF16)
        give(1, c)

    for phase in range(2):
        for c in range(chunks):
            sent = xin.at[pl.ds(2 * phase, 2), pl.ds(0, (peers - 1) * rows), pl.ds(c * span, span)]
            pltpu.make_async_copy(sent, sent, in_send.at[phase, c]).wait()
            pltpu.make_async_copy(sent, sent, out_send.at[phase, c]).wait()
            whole = xout.at[pl.ds(2 * phase, 2), :, pl.ds(c * span, span)]
            pltpu.make_async_copy(whole, whole, out_recv.at[phase, c]).wait()
    for c in range(chunks):
        @pl.when(group < n_groups - 1)
        def _(c=c):
            state_copy(psend, pin, p_send, p_recv, c, later).wait_send()

        @pl.when(group > 0)
        def _(c=c):
            state_copy(ssend, sin, s_send, s_recv, c, earlier).wait_send()


def per_device(mesh, query, key, value, cotangent, gain, incoming_state):
    n_seq, n_head = mesh.shape["seq"], mesh.shape["head"]
    rows, features = query.shape
    local_heads = incoming_state.shape[0]
    sub = 1
    while sub < 4 and n_seq % (2 * sub) == 0 and local_heads % (2 * sub) == 0:
        sub *= 2
    heads = local_heads // sub
    step = max(1, heads // 4)
    chunks = heads // step
    tokens = rows * n_head * sub
    width = heads * HEAD_DIM
    plan = (n_seq // sub, sub, n_head, rows, heads, step)
    anywhere = pl.BlockSpec(memory_space=pl.ANY)
    resident = pl.BlockSpec(memory_space=pltpu.HBM)
    state = pltpu.VMEM((heads, HEAD_DIM, HEAD_DIM), F32)
    states = pltpu.VMEM((heads, sub, HEAD_DIM, HEAD_DIM), F32)
    sems = pltpu.SemaphoreType.DMA((2, chunks))
    chain = pltpu.SemaphoreType.DMA((chunks,))
    return pl.pallas_call(
        functools.partial(kernel, plan),
        out_shape=[jax.ShapeDtypeStruct((rows, features), BF16)] * 4,
        in_specs=[resident] * 6,
        out_specs=[anywhere] * 4,
        scratch_shapes=[
            pltpu.VMEM((4, tokens, width), BF16),
            pltpu.VMEM((4, tokens, width), BF16),
            pltpu.VMEM((2, tokens, width), F32),
            states, states, state, state, state, state, state,
            pltpu.VMEM((local_heads, HEAD_DIM), F32),
            sems, sems, sems, sems, chain, chain, chain, chain,
            pltpu.SemaphoreType.DMA,
        ],
        compiler_params=pltpu.CompilerParams(
            collective_id=0, has_side_effects=True, vmem_limit_bytes=51000 * 1024),
    )(query, key, value, cotangent, gain.reshape(local_heads, HEAD_DIM), incoming_state)


def solution(mesh):
    tokens = P(("seq", "head"), None)
    return jax.shard_map(
        functools.partial(per_device, mesh),
        mesh=mesh,
        in_specs=(tokens, tokens, tokens, tokens, P("head"), P("head", None, None)),
        out_specs=(tokens, tokens, tokens, tokens),
        check_vma=False,
    )
```

profile of v0, /device:TPU:0, one launch (start us, length us, event | category | flops | bytes accessed | tf_op | source)
XLA Modules:
  0.0 100.2 jit_solution(7546822344428470009)
XLA Ops:
  0.6 0.0 copy-start
  0.6 0.7 copy-done
  1.4 95.0 %shard_map.93 = (bf16[64,8192]{1,0:T(8,128)(2,1)S(1)}, bf16[64,8192]{1,0:T(8,128)(2,1)S(1)}, bf16[64,8192]{1,0:T(8,128)(2,1)S(1)}, bf16[64,8192]{1,0:T(8,128)(2,1)S(1)}) custom-call(bf16[64,8192]{1,0:T(8,128)(2,1)} %q_hbm.1, bf16[64,8192]{1,0:T(8,128)(2,1)} %k_hbm.1, bf16[64,8192]{1,0:T(8,128)(2,1)} %v_hbm.1, bf16[64,8192]{1,0:T(8,128)(2,1)} %y_hbm.1, ...), custom_call_target="tpu_custom_call" | custom-call | tf_op jit(solution)/shard_map/pallas_call | solution.py:291
  96.3 1.0 copy.14
  97.3 1.0 copy.15
  98.3 1.0 copy.16
  99.2 1.0 copy.17
Async XLA Ops:
  0.6 0.7 copy-start
where the time goes:
time: 101 us; the launch traced here: 100 us
  Pallas kernels  95 us (94%)
  local copies, waits for them, and re-layouts  4.59 us (5%)
    pallas_call x1, Pallas kernels, per_device(): pl.pallas_call(functools.partial(kernel, plan), out_shape=[jax.ShapeDtype...  95 us
    unnamed x6, local copies, waits for them, and re-layouts  4.59 us

commit v1 on v0

--- a/solution.py
+++ b/solution.py
@@ -269,6 +269,19 @@
             state_copy(ssend, sin, s_send, s_recv, c, earlier).wait_send()
 
 
+def land(parts, *refs):
+    sources, targets, sem = refs[:4], refs[4:8], refs[8]
+    copies = []
+    rows = sources[0].shape[0] // parts
+    for part in range(parts):
+        for src, dst in zip(sources, targets):
+            piece = pl.ds(part * rows, rows)
+            copies.append(pltpu.make_async_copy(src.at[piece], dst.at[piece], sem))
+            copies[-1].start()
+    for copy in copies:
+        copy.wait()
+
+
 def per_device(mesh, query, key, value, cotangent, gain, incoming_state):
     n_seq, n_head = mesh.shape["seq"], mesh.shape["head"]
     rows, features = query.shape
@@ -288,9 +301,10 @@
     states = pltpu.VMEM((heads, sub, HEAD_DIM, HEAD_DIM), F32)
     sems = pltpu.SemaphoreType.DMA((2, chunks))
     chain = pltpu.SemaphoreType.DMA((chunks,))
-    return pl.pallas_call(
+    shapes = [jax.ShapeDtypeStruct((rows, features), BF16)] * 4
+    results = pl.pallas_call(
         functools.partial(kernel, plan),
-        out_shape=[jax.ShapeDtypeStruct((rows, features), BF16)] * 4,
+        out_shape=shapes,
         in_specs=[resident] * 6,
         out_specs=[anywhere] * 4,
         scratch_shapes=[
@@ -305,6 +319,14 @@
         compiler_params=pltpu.CompilerParams(
             collective_id=0, has_side_effects=True, vmem_limit_bytes=51000 * 1024),
     )(query, key, value, cotangent, gain.reshape(local_heads, HEAD_DIM), incoming_state)
+    return pl.pallas_call(
+        functools.partial(land, 4 if rows % 64 == 0 else 1),
+        out_shape=shapes,
+        in_specs=[anywhere] * 4,
+        out_specs=[anywhere] * 4,
+        scratch_shapes=[pltpu.SemaphoreType.DMA],
+        compiler_params=pltpu.CompilerParams(vmem_limit_bytes=1024 * 1024),
+    )(*results)
 
 
 def solution(mesh):

time: 101 us -> 98.9 us (0.979)
  local copies, waits for them, and re-layouts: 4.59 us -> 0.71 us
  Pallas kernels: 95 us -> 97 us
    unnamed x6 -> x2, local copies, waits for them, and re-layouts: 4.59 us -> 0.71 us
    pallas_call x1 -> x2, Pallas kernels: 95 us -> 97 us  [the longest x1 95 us: per_device(): pl.pallas_call(functools.partial(kernel, plan), out_shape=shapes, in_spec...]
where the time goes in v1:
time: 98.9 us; the launch traced here: 98.3 us
  Pallas kernels  97 us (98%)
    pallas_call x1, Pallas kernels, per_device(): pl.pallas_call(functools.partial(kernel, plan), out_shape=shapes, in_spec...  95 us
    pallas_call x1, Pallas kernels, per_device(): pl.pallas_call(functools.partial(land, 4 if rows % 64 == 0 else 1), out_s...  2 us

profile of v1, /device:TPU:0, one launch (start us, length us, event | category | flops | bytes accessed | tf_op | source)
XLA Modules:
  0.0 98.3 jit_solution(2183465673599989821)
XLA Ops:
  0.6 0.0 copy-start
  0.6 0.7 copy-done
  1.4 95.0 %shard_map.93 = (bf16[64,8192]{1,0:T(8,128)(2,1)S(1)}, bf16[64,8192]{1,0:T(8,128)(2,1)S(1)}, bf16[64,8192]{1,0:T(8,128)(2,1)S(1)}, bf16[64,8192]{1,0:T(8,128)(2,1)S(1)}) custom-call(bf16[64,8192]{1,0:T(8,128)(2,1)} %q_hbm.1, bf16[64,8192]{1,0:T(8,128)(2,1)} %k_hbm.1, bf16[64,8192]{1,0:T(8,128)(2,1)} %v_hbm.1, bf16[64,8192]{1,0:T(8,128)(2,1)} %y_hbm.1, ...), custom_call_target="tpu_custom_call" | custom-call | tf_op jit(solution)/shard_map/pallas_call | solution.py:305
  96.3 2.0 %shard_map.94 = (bf16[64,8192]{1,0:T(8,128)(2,1)}, bf16[64,8192]{1,0:T(8,128)(2,1)}, bf16[64,8192]{1,0:T(8,128)(2,1)}, bf16[64,8192]{1,0:T(8,128)(2,1)}) custom-call(bf16[64,8192]{1,0:T(8,128)(2,1)S(1)} %get-tuple-element.8.refs_0_, bf16[64,8192]{1,0:T(8,128)(2,1)S(1)} %get-tuple-element.9.refs_1_, bf16[64,8192]{1,0:T(8,128)(2,1)S(1)} %get-tuple-element.10.refs_2_, ...), custom_call_target="tpu_custom_call" | custom-call | tf_op jit(solution)/shard_map/pallas_call | solution.py:322
Async XLA Ops:
  0.6 0.7 copy-start

commit v2 on v1

v2 whole, which is shorter than its diff:
```python
import functools

import jax
import jax.numpy as jnp
from jax import lax
from jax.experimental import pallas as pl
from jax.experimental.pallas import tpu as pltpu
from jax.sharding import PartitionSpec as P

HEAD_DIM = 128
EPSILON = 1e-06
MESH = pl.DeviceIdType.MESH
F32 = jnp.float32
BF16 = jnp.bfloat16

NT = (((1,), (1,)), ((), ()))
TN = (((0,), (0,)), ((), ()))
NN = (((1,), (0,)), ((), ()))


def dot(a, b, dims):
    return lax.dot_general(a, b, dims, preferred_element_type=F32)


def kernel(plan, q_hbm, k_hbm, v_hbm, y_hbm, gain_hbm, s0_hbm, o_out, gq_out, gk_out, gv_out,
           xin, xout, part, cum, gcum, prefix, tot, gtot, xt, xg, pin, psend, sin, ssend, gain,
           in_send, in_recv, out_send, out_recv, p_send, p_recv, s_send, s_recv,
           t_send, t_recv, g_send, g_recv, gain_sem, ready):
    n_outer, n_inner, sub, n_head, rows, heads, step = plan
    peers = sub * n_head
    chunks = heads // step
    block = rows * n_head
    span = step * HEAD_DIM
    seq, hd = lax.axis_index("seq"), lax.axis_index("head")
    group, j = seq // sub, lax.rem(seq, sub)
    outer, inner = group // n_inner, lax.rem(group, n_inner)
    me = j * n_head + hd

    def place(p):
        to_j = lax.rem(j + p // n_head, sub)
        to_hd = lax.rem(hd + lax.rem(p, n_head), n_head)
        return to_j * n_head + to_hd, (group * sub + to_j, to_hd)

    def column(other, c):
        owner = lax.rem(other, n_head) * (sub * heads) + (other // n_head) * heads + c * step
        return pl.ds(pl.multiple_of(owner * HEAD_DIM, span), span)

    def strip(index):
        return pl.ds(pl.multiple_of(index * rows, rows), rows)

    def cols(c):
        return pl.ds(pl.multiple_of(c * span, span), span)

    def piece(c):
        return pl.ds(c * step, step)

    across = ((outer * n_inner + (n_inner - 1 - inner)) * sub + j, hd)
    later = (seq + n_inner * sub, hd)
    earlier = (seq - n_inner * sub, hd)
    first, last = outer == 0, outer == n_outer - 1
    barrier = pltpu.get_barrier_semaphore()

    def greet(p, carry):
        _, device = place(p)
        pl.semaphore_signal(barrier, inc=1, device_id=device, device_id_type=MESH)
        return carry

    lax.fori_loop(1, peers, greet, 0)
    inside = inner == 0

    if n_inner == 2:
        @pl.when(inside)
        def _():
            pl.semaphore_signal(barrier, inc=1, device_id=across, device_id_type=MESH)

    @pl.when(jnp.logical_not(last))
    def _():
        pl.semaphore_signal(barrier, inc=1, device_id=later, device_id_type=MESH)

    sources = ((k_hbm, v_hbm), (q_hbm, y_hbm))
    targets = ((o_out, gq_out), (gk_out, gv_out))

    for more_x in range(n_inner):
        for more_z in range(2):
            @pl.when(jnp.logical_and(inner == more_x, first == (more_z == 0)))
            def _(more=more_x + more_z):
                pl.semaphore_wait(barrier, peers - 1 + more)

    for phase in range(2):
        def scatter(c, carry, phase=phase):
            def one(p, carry):
                other, device = place(p)
                for a in range(2):
                    pltpu.make_async_remote_copy(
                        src_ref=sources[phase][a].at[:, column(other, c)],
                        dst_ref=xin.at[2 * phase + a, strip(me), cols(c)],
                        send_sem=in_send.at[phase, c],
                        recv_sem=in_recv.at[phase, c],
                        device_id=device,
                        device_id_type=MESH,
                    ).start()
                return carry

            lax.fori_loop(1, peers, one, 0)
            for a in range(2):
                pltpu.make_async_copy(
                    sources[phase][a].at[:, column(me, c)],
                    xin.at[2 * phase + a, strip(me), cols(c)],
                    in_recv.at[phase, c],
                ).start()
            return carry

        lax.fori_loop(0, chunks, scatter, 0)

    gains = pltpu.make_async_copy(gain_hbm, gain, gain_sem)
    gains.start()

    if n_inner == 2:
        @pl.when(jnp.logical_not(inside))
        def _():
            pl.semaphore_signal(ready.at[0], inc=1, device_id=across, device_id_type=MESH)

    @pl.when(jnp.logical_not(first))
    def _():
        pl.semaphore_signal(ready.at[1], inc=1, device_id=earlier, device_id_type=MESH)

    @pl.when(first)
    def _():
        def carried_in(c, carry):
            pltpu.make_async_copy(
                s0_hbm.at[pl.ds(j * heads + c * step, step)], pin.at[piece(c)], p_recv.at[c],
            ).start()
            return carry

        lax.fori_loop(0, chunks, carried_in, 0)

    @pl.when(last)
    def _():
        sin[...] = jnp.zeros_like(sin)

    row = lax.broadcasted_iota(jnp.int32, (block, block), 0)
    col = lax.broadcasted_iota(jnp.int32, (block, block), 1)
    causal = col <= row
    gains.wait()

    if n_inner == 2:
        @pl.when(inside)
        def _():
            pl.semaphore_wait(ready.at[0], 1)

    @pl.when(jnp.logical_not(last))
    def _():
        pl.semaphore_wait(ready.at[1], 1)

    def arrived(phase, c):
        ref = xin.at[pl.ds(2 * phase, 2), :, cols(c)]
        pltpu.make_async_copy(ref, ref, in_recv.at[phase, c]).wait()

    def give(phase, c):
        def back(p, carry):
            other, device = place(p)
            for a in range(2):
                pltpu.make_async_remote_copy(
                    src_ref=xout.at[2 * phase + a, strip(other), cols(c)],
                    dst_ref=targets[phase][a].at[:, column(me, c)],
                    send_sem=out_send.at[phase, c],
                    recv_sem=out_recv.at[phase, c],
                    device_id=device,
                    device_id_type=MESH,
                ).start()
            return carry

        lax.fori_loop(1, peers, back, 0)
        for a in range(2):
            pltpu.make_async_copy(
                xout.at[2 * phase + a, strip(me), cols(c)],
                targets[phase][a].at[:, column(me, c)],
                out_recv.at[phase, c],
            ).start()

    def state_copy(src, dst, send, recv, c, device):
        return pltpu.make_async_remote_copy(
            src_ref=src.at[piece(c)], dst_ref=dst.at[piece(c)], send_sem=send.at[c],
            recv_sem=recv.at[c], device_id=device, device_id_type=MESH)

    def landed(ref, recv, c):
        pltpu.make_async_copy(ref.at[piece(c)], ref.at[piece(c)], recv.at[c]).wait()

    def lanes(c, h):
        return pl.ds(pl.multiple_of(c * span + h * HEAD_DIM, HEAD_DIM), HEAD_DIM)

    def block_states(c):
        arrived(0, c)
        for h in range(step):
            n, hc = c * step + h, lanes(c, h)
            run = dot(xin[0, :block, hc], xin[1, :block, hc], TN)
            for b in range(1, sub):
                r = slice(b * block, (b + 1) * block)
                cum[n, b - 1] = run
                run = run + dot(xin[0, r, hc], xin[1, r, hc], TN)
            tot[n] = run
        if n_inner == 2:
            state_copy(tot, xt, t_send, t_recv, c, across).start()

    def pass_prefix(c):
        if n_inner == 2:
            landed(xt, t_recv, c)
        landed(pin, p_recv, c)

        @pl.when(jnp.logical_not(last))
        def _():
            for h in range(step):
                n = c * step + h
                psend[n] = pin[n] + tot[n] + xt[n] if n_inner == 2 else pin[n] + tot[n]
            state_copy(psend, pin, p_send, p_recv, c, later).start()

        for h in range(step):
            n = c * step + h
            before = pin[n]
            if n_inner == 2:
                before = before + jnp.where(inner == 1, xt[n], 0.0)
            prefix[n, 0] = before.astype(BF16)
            for b in range(1, sub):
                prefix[n, b] = (before + cum[n, b - 1]).astype(BF16)

    def attend(c):
        arrived(1, c)
        for h in range(step):
            n, hc = c * step + h, lanes(c, h)
            at = pl.multiple_of((j * heads + n) * HEAD_DIM, HEAD_DIM)
            g = gain[pl.ds(at, HEAD_DIM)].reshape(1, HEAD_DIM)
            run = None
            for b in reversed(range(sub)):
                r = slice(b * block, (b + 1) * block)
                k, v, q, up = xin[0, r, hc], xin[1, r, hc], xin[2, r, hc], xin[3, r, hc]
                state = prefix[n, b]
                w = jnp.where(causal, dot(q, k, NT), 0.0).astype(BF16)
                att = dot(w, v, NN) + dot(q, state, NN)
                inv = lax.rsqrt(jnp.mean(att * att, axis=-1, keepdims=True) + EPSILON)
                normed = att * inv
                xout[0, r, hc] = (normed * g).astype(BF16)
                scaled = up.astype(F32) * g
                ga = ((scaled - normed * jnp.mean(scaled * normed, axis=-1, keepdims=True))
                      * inv).astype(BF16)
                gw = jnp.where(causal, dot(ga, v, NT), 0.0).astype(BF16)
                xout[1, r, hc] = (dot(gw, k, NN) + dot(ga, state, NT)).astype(BF16)
                part[0, r, hc] = dot(gw, q, TN)
                part[1, r, hc] = dot(w, ga, TN)
                if run is not None:
                    gcum[n, b] = run
                grad = dot(q, ga, TN)
                run = grad if run is None else run + grad
            gtot[n] = run
        if n_inner == 2:
            state_copy(gtot, xg, g_send, g_recv, c, across).start()
        give(0, c)

    def finish(c):
        if n_inner == 2:
            landed(xg, g_recv, c)

        @pl.when(jnp.logical_not(last))
        def _():
            landed(sin, s_recv, c)

        @pl.when(jnp.logical_not(first))
        def _():
            for h in range(step):
                n = c * step + h
                ssend[n] = sin[n] + gtot[n] + xg[n] if n_inner == 2 else sin[n] + gtot[n]
            state_copy(ssend, sin, s_send, s_recv, c, earlier).start()

        for h in range(step):
            n, hc = c * step + h, lanes(c, h)
            after = sin[n]
            if n_inner == 2:
                after = after + jnp.where(inner == 0, xg[n], 0.0)
            for b in range(sub):
                r = slice(b * block, (b + 1) * block)
                suffix = (after + gcum[n, b] if b < sub - 1 else after).astype(BF16)
                xout[2, r, hc] = (part[0, r, hc] + dot(xin[1, r, hc], suffix, NT)).astype(BF16)
                xout[3, r, hc] = (part[1, r, hc] + dot(xin[0, r, hc], suffix, NN)).astype(BF16)
        give(1, c)

    prefix_lag = jnp.minimum(2 + 2 * outer, chunks)
    suffix_lag = chunks + 2 + 2 * (n_outer - 1 - outer)

    def tick(i, carry):
        @pl.when(i < chunks)
        def _():
            block_states(i)

        @pl.when(jnp.logical_and(i >= prefix_lag, i < prefix_lag + chunks))
        def _():
            pass_prefix(i - prefix_lag)

        @pl.when(jnp.logical_and(i >= chunks, i < 2 * chunks))
        def _():
            attend(i - chunks)

        @pl.when(jnp.logical_and(i >= suffix_lag, i < suffix_lag + chunks))
        def _():
            finish(i - suffix_lag)

        return carry

    lax.fori_loop(0, 2 * chunks + 2 * n_outer, tick, 0)

    def drain(c, carry):
        for phase in range(2):
            sent = xin.at[pl.ds(2 * phase, 2), pl.ds(0, (peers - 1) * rows), cols(c)]
            pltpu.make_async_copy(sent, sent, in_send.at[phase, c]).wait()
            pltpu.make_async_copy(sent, sent, out_send.at[phase, c]).wait()
            whole = xout.at[pl.ds(2 * phase, 2), :, cols(c)]
            pltpu.make_async_copy(whole, whole, out_recv.at[phase, c]).wait()
        if n_inner == 2:
            state_copy(tot, xt, t_send, t_recv, c, across).wait_send()
            state_copy(gtot, xg, g_send, g_recv, c, across).wait_send()

        @pl.when(jnp.logical_not(last))
        def _():
            state_copy(psend, pin, p_send, p_recv, c, later).wait_send()

        @pl.when(jnp.logical_not(first))
        def _():
            state_copy(ssend, sin, s_send, s_recv, c, earlier).wait_send()

        return carry

    lax.fori_loop(0, chunks, drain, 0)


def land(parts, *refs):
    sources, targets, sem = refs[:4], refs[4:8], refs[8]
    copies = []
    rows = sources[0].shape[0] // parts
    for part in range(parts):
        for src, dst in zip(sources, targets):
            piece = pl.ds(part * rows, rows)
            copies.append(pltpu.make_async_copy(src.at[piece], dst.at[piece], sem))
            copies[-1].start()
    for copy in copies:
        copy.wait()


def per_device(mesh, query, key, value, cotangent, gain, incoming_state):
    n_seq, n_head = mesh.shape["seq"], mesh.shape["head"]
    rows, features = query.shape
    local_heads = incoming_state.shape[0]
    sub = 2 if n_seq % 2 == 0 and local_heads % 2 == 0 else 1
    n_inner = 2 if n_seq % (2 * sub) == 0 else 1
    n_outer = n_seq // (sub * n_inner)
    heads = local_heads // sub
    step = next(s for s in range(max(1, heads // 8), heads + 1) if heads % s == 0)
    chunks = heads // step
    tokens = rows * n_head * sub
    width = heads * HEAD_DIM
    plan = (n_outer, n_inner, sub, n_head, rows, heads, step)
    anywhere = pl.BlockSpec(memory_space=pl.ANY)
    resident = pl.BlockSpec(memory_space=pltpu.HBM)
    state = pltpu.VMEM((heads, HEAD_DIM, HEAD_DIM), F32)
    states = pltpu.VMEM((heads, max(1, sub - 1), HEAD_DIM, HEAD_DIM), F32)
    sems = pltpu.SemaphoreType.DMA((2, chunks))
    chain = pltpu.SemaphoreType.DMA((chunks,))
    shapes = [jax.ShapeDtypeStruct((rows, features), BF16)] * 4
    results = pl.pallas_call(
        functools.partial(kernel, plan),
        out_shape=shapes,
        in_specs=[resident] * 6,
        out_specs=[anywhere] * 4,
        scratch_shapes=[
            pltpu.VMEM((4, tokens, width), BF16),
            pltpu.VMEM((4, tokens, width), BF16),
            pltpu.VMEM((2, tokens, width), F32),
            states, states,
            pltpu.VMEM((heads, sub, HEAD_DIM, HEAD_DIM), BF16),
            state, state, state, state, state, state, state, state,
            pltpu.VMEM((local_heads * HEAD_DIM,), F32),
            sems, sems, sems, sems, chain, chain, chain, chain, chain, chain, chain, chain,
            pltpu.SemaphoreType.DMA, pltpu.SemaphoreType.REGULAR((2,)),
        ],
        compiler_params=pltpu.CompilerParams(
            collective_id=0, has_side_effects=True, vmem_limit_bytes=51000 * 1024),
    )(query, key, value, cotangent, pltpu.with_memory_space_constraint(gain, pltpu.HBM),
      incoming_state)
    return pl.pallas_call(
        functools.partial(land, 4 if rows % 64 == 0 else 1),
        out_shape=shapes,
        in_specs=[anywhere] * 4,
        out_specs=[anywhere] * 4,
        scratch_shapes=[pltpu.SemaphoreType.DMA],
        compiler_params=pltpu.CompilerParams(vmem_limit_bytes=1024 * 1024),
    )(*results)


def solution(mesh):
    tokens = P(("seq", "head"), None)
    return jax.shard_map(
        functools.partial(per_device, mesh),
        mesh=mesh,
        in_specs=(tokens, tokens, tokens, tokens, P("head"), P("head", None, None)),
        out_specs=(tokens, tokens, tokens, tokens),
        check_vma=False,
    )
```

time: 98.9 us -> 98.2 us (level)
  no operation moved by 1% of the time
where the time goes in v2:
time: 98.2 us; the launch traced here: 98.1 us
  Pallas kernels  97.4 us (99%)
    pallas_call x1, Pallas kernels, per_device(): pl.pallas_call(functools.partial(kernel, plan), out_shape=shapes, in_spec...  95.4 us
    pallas_call x1, Pallas kernels, per_device(): pl.pallas_call(functools.partial(land, 4 if rows % 64 == 0 else 1), out_s...  2 us

profile of v2, /device:TPU:0, one launch (start us, length us, event | category | flops | bytes accessed | tf_op | source)
XLA Modules:
  0.0 98.1 jit_solution(8108072489201012212)
XLA Ops:
  0.6 95.4 %shard_map.93 = (bf16[64,8192]{1,0:T(8,128)(2,1)S(1)}, bf16[64,8192]{1,0:T(8,128)(2,1)S(1)}, bf16[64,8192]{1,0:T(8,128)(2,1)S(1)}, bf16[64,8192]{1,0:T(8,128)(2,1)S(1)}) custom-call(bf16[64,8192]{1,0:T(8,128)(2,1)} %q_hbm.1, bf16[64,8192]{1,0:T(8,128)(2,1)} %k_hbm.1, bf16[64,8192]{1,0:T(8,128)(2,1)} %v_hbm.1, bf16[64,8192]{1,0:T(8,128)(2,1)} %y_hbm.1, ...), custom_call_target="tpu_custom_call" | custom-call | tf_op jit(solution)/shard_map/pallas_call | solution.py:366
  96.1 2.0 %shard_map.94 = (bf16[64,8192]{1,0:T(8,128)(2,1)}, bf16[64,8192]{1,0:T(8,128)(2,1)}, bf16[64,8192]{1,0:T(8,128)(2,1)}, bf16[64,8192]{1,0:T(8,128)(2,1)}) custom-call(bf16[64,8192]{1,0:T(8,128)(2,1)S(1)} %get-tuple-element.8.refs_0_, bf16[64,8192]{1,0:T(8,128)(2,1)S(1)} %get-tuple-element.9.refs_1_, bf16[64,8192]{1,0:T(8,128)(2,1)S(1)} %get-tuple-element.10.refs_2_, ...), custom_call_target="tpu_custom_call" | custom-call | tf_op jit(solution)/shard_map/pallas_call | solution.py:386

commit v3 on v2

--- a/solution.py
+++ b/solution.py
@@ -24,8 +24,8 @@
 
 def kernel(plan, q_hbm, k_hbm, v_hbm, y_hbm, gain_hbm, s0_hbm, o_out, gq_out, gk_out, gv_out,
            xin, xout, part, cum, gcum, prefix, tot, gtot, xt, xg, pin, psend, sin, ssend, gain,
-           in_send, in_recv, out_send, out_recv, p_send, p_recv, s_send, s_recv,
-           t_send, t_recv, g_send, g_recv, gain_sem, ready):
+           in_recv, chain_recv, t_recv, g_recv, in_send, out_send, out_recv,
+           p_send, s_send, t_send, g_send, gain_sem, ready):
     n_outer, n_inner, sub, n_head, rows, heads, step = plan
     peers = sub * n_head
     chunks = heads // step
@@ -94,7 +94,7 @@
                     pltpu.make_async_remote_copy(
                         src_ref=sources[phase][a].at[:, column(other, c)],
                         dst_ref=xin.at[2 * phase + a, strip(me), cols(c)],
-                        send_sem=in_send.at[phase, c],
+                        send_sem=in_send,
                         recv_sem=in_recv.at[phase, c],
                         device_id=device,
                         device_id_type=MESH,
@@ -128,7 +128,7 @@
     def _():
         def carried_in(c, carry):
             pltpu.make_async_copy(
-                s0_hbm.at[pl.ds(j * heads + c * step, step)], pin.at[piece(c)], p_recv.at[c],
+                s0_hbm.at[pl.ds(j * heads + c * step, step)], pin.at[piece(c)], chain_recv.at[c],
             ).start()
             return carry
 
@@ -163,8 +163,8 @@
                 pltpu.make_async_remote_copy(
                     src_ref=xout.at[2 * phase + a, strip(other), cols(c)],
                     dst_ref=targets[phase][a].at[:, column(me, c)],
-                    send_sem=out_send.at[phase, c],
-                    recv_sem=out_recv.at[phase, c],
+                    send_sem=out_send,
+                    recv_sem=out_recv,
                     device_id=device,
                     device_id_type=MESH,
                 ).start()
@@ -175,12 +175,12 @@
             pltpu.make_async_copy(
                 xout.at[2 * phase + a, strip(me), cols(c)],
                 targets[phase][a].at[:, column(me, c)],
-                out_recv.at[phase, c],
+                out_recv,
             ).start()
 
     def state_copy(src, dst, send, recv, c, device):
         return pltpu.make_async_remote_copy(
-            src_ref=src.at[piece(c)], dst_ref=dst.at[piece(c)], send_sem=send.at[c],
+            src_ref=src.at[piece(c)], dst_ref=dst.at[piece(c)], send_sem=send,
             recv_sem=recv.at[c], device_id=device, device_id_type=MESH)
 
     def landed(ref, recv, c):
@@ -205,14 +205,14 @@
     def pass_prefix(c):
         if n_inner == 2:
             landed(xt, t_recv, c)
-        landed(pin, p_recv, c)
+        landed(pin, chain_recv, c)
 
         @pl.when(jnp.logical_not(last))
         def _():
             for h in range(step):
                 n = c * step + h
                 psend[n] = pin[n] + tot[n] + xt[n] if n_inner == 2 else pin[n] + tot[n]
-            state_copy(psend, pin, p_send, p_recv, c, later).start()
+            state_copy(psend, pin, p_send, chain_recv, c, later).start()
 
         for h in range(step):
             n = c * step + h
@@ -261,14 +261,14 @@
 
         @pl.when(jnp.logical_not(last))
         def _():
-            landed(sin, s_recv, c)
+            landed(sin, chain_recv, c)
 
         @pl.when(jnp.logical_not(first))
         def _():
             for h in range(step):
                 n = c * step + h
                 ssend[n] = sin[n] + gtot[n] + xg[n] if n_inner == 2 else sin[n] + gtot[n]
-            state_copy(ssend, sin, s_send, s_recv, c, earlier).start()
+            state_copy(ssend, sin, s_send, chain_recv, c, earlier).start()
 
         for h in range(step):
             n, hc = c * step + h, lanes(c, h)
@@ -306,28 +306,22 @@
 
     lax.fori_loop(0, 2 * chunks + 2 * n_outer, tick, 0)
 
-    def drain(c, carry):
-        for phase in range(2):
-            sent = xin.at[pl.ds(2 * phase, 2), pl.ds(0, (peers - 1) * rows), cols(c)]
-            pltpu.make_async_copy(sent, sent, in_send.at[phase, c]).wait()
-            pltpu.make_async_copy(sent, sent, out_send.at[phase, c]).wait()
-            whole = xout.at[pl.ds(2 * phase, 2), :, cols(c)]
-            pltpu.make_async_copy(whole, whole, out_recv.at[phase, c]).wait()
-        if n_inner == 2:
-            state_copy(tot, xt, t_send, t_recv, c, across).wait_send()
-            state_copy(gtot, xg, g_send, g_recv, c, across).wait_send()
-
-        @pl.when(jnp.logical_not(last))
-        def _():
-            state_copy(psend, pin, p_send, p_recv, c, later).wait_send()
-
-        @pl.when(jnp.logical_not(first))
-        def _():
-            state_copy(ssend, sin, s_send, s_recv, c, earlier).wait_send()
-
-        return carry
-
-    lax.fori_loop(0, chunks, drain, 0)
+    sent = xin.at[:, pl.ds(0, (peers - 1) * rows)]
+    pltpu.make_async_copy(sent, sent, in_send).wait()
+    pltpu.make_async_copy(sent, sent, out_send).wait()
+    if n_inner == 2:
+        pltpu.make_async_copy(tot, tot, t_send).wait()
+        pltpu.make_async_copy(gtot, gtot, g_send).wait()
+
+    @pl.when(jnp.logical_not(last))
+    def _():
+        pltpu.make_async_copy(psend, psend, p_send).wait()
+
+    @pl.when(jnp.logical_not(first))
+    def _():
+        pltpu.make_async_copy(ssend, ssend, s_send).wait()
+
+    pltpu.make_async_copy(xout, xout, out_recv).wait()
 
 
 def land(parts, *refs):
@@ -362,6 +356,7 @@
     states = pltpu.VMEM((heads, max(1, sub - 1), HEAD_DIM, HEAD_DIM), F32)
     sems = pltpu.SemaphoreType.DMA((2, chunks))
     chain = pltpu.SemaphoreType.DMA((chunks,))
+    one = pltpu.SemaphoreType.DMA
     shapes = [jax.ShapeDtypeStruct((rows, features), BF16)] * 4
     results = pl.pallas_call(
         functools.partial(kernel, plan),
@@ -376,8 +371,8 @@
             pltpu.VMEM((heads, sub, HEAD_DIM, HEAD_DIM), BF16),
             state, state, state, state, state, state, state, state,
             pltpu.VMEM((local_heads * HEAD_DIM,), F32),
-            sems, sems, sems, sems, chain, chain, chain, chain, chain, chain, chain, chain,
-            pltpu.SemaphoreType.DMA, pltpu.SemaphoreType.REGULAR((2,)),
+            sems, chain, chain, chain, one, one, one, one, one, one, one, one,
+            pltpu.SemaphoreType.REGULAR((2,)),
         ],
         compiler_params=pltpu.CompilerParams(
             collective_id=0, has_side_effects=True, vmem_limit_bytes=51000 * 1024),

time: 98.2 us -> 97.5 us (level)
  no operation moved by 1% of the time
where the time goes in v3:
time: 97.5 us; the launch traced here: 97.3 us
  Pallas kernels  96.7 us (99%)
    pallas_call x1, Pallas kernels, per_device(): pl.pallas_call(functools.partial(kernel, plan), out_shape=shapes, in_spec...  94.7 us
    pallas_call x1, Pallas kernels, per_device(): pl.pallas_call(functools.partial(land, 4 if rows % 64 == 0 else 1), out_s...  2 us

profile of v3, /device:TPU:0, one launch (start us, length us, event | category | flops | bytes accessed | tf_op | source)
XLA Modules:
  0.0 97.3 jit_solution(5838115660210628188)
XLA Ops:
  0.6 94.7 %shard_map.93 = (bf16[64,8192]{1,0:T(8,128)(2,1)S(1)}, bf16[64,8192]{1,0:T(8,128)(2,1)S(1)}, bf16[64,8192]{1,0:T(8,128)(2,1)S(1)}, bf16[64,8192]{1,0:T(8,128)(2,1)S(1)}) custom-call(bf16[64,8192]{1,0:T(8,128)(2,1)} %q_hbm.1, bf16[64,8192]{1,0:T(8,128)(2,1)} %k_hbm.1, bf16[64,8192]{1,0:T(8,128)(2,1)} %v_hbm.1, bf16[64,8192]{1,0:T(8,128)(2,1)} %y_hbm.1, ...), custom_call_target="tpu_custom_call" | custom-call | tf_op jit(solution)/shard_map/pallas_call | solution.py:361
  95.3 2.0 %shard_map.94 = (bf16[64,8192]{1,0:T(8,128)(2,1)}, bf16[64,8192]{1,0:T(8,128)(2,1)}, bf16[64,8192]{1,0:T(8,128)(2,1)}, bf16[64,8192]{1,0:T(8,128)(2,1)}) custom-call(bf16[64,8192]{1,0:T(8,128)(2,1)S(1)} %get-tuple-element.8.refs_0_, bf16[64,8192]{1,0:T(8,128)(2,1)S(1)} %get-tuple-element.9.refs_1_, bf16[64,8192]{1,0:T(8,128)(2,1)S(1)} %get-tuple-element.10.refs_2_, ...), custom_call_target="tpu_custom_call" | custom-call | tf_op jit(solution)/shard_map/pallas_call | solution.py:381

commit v4 on v3

--- a/solution.py
+++ b/solution.py
@@ -9,6 +9,7 @@
 
 HEAD_DIM = 128
 EPSILON = 1e-06
+DETOUR_ARRAYS, DETOUR_CHUNKS = 1, 1
 MESH = pl.DeviceIdType.MESH
 F32 = jnp.float32
 BF16 = jnp.bfloat16
@@ -23,9 +24,9 @@
 
 
 def kernel(plan, q_hbm, k_hbm, v_hbm, y_hbm, gain_hbm, s0_hbm, o_out, gq_out, gk_out, gv_out,
-           xin, xout, part, cum, gcum, prefix, tot, gtot, xt, xg, pin, psend, sin, ssend, gain,
+           xin, xout, part, cum, gcum, prefix, tot, gtot, xt, xg, pin, psend, sin, ssend, gain, hop,
            in_recv, chain_recv, t_recv, g_recv, in_send, out_send, out_recv,
-           p_send, s_send, t_send, g_send, gain_sem, ready):
+           p_send, s_send, t_send, g_send, gain_sem, hop_send, hop_recv, ready):
     n_outer, n_inner, sub, n_head, rows, heads, step = plan
     peers = sub * n_head
     chunks = heads // step
@@ -58,6 +59,12 @@
     later = (seq + n_inner * sub, hd)
     earlier = (seq - n_inner * sub, hd)
     first, last = outer == 0, outer == n_outer - 1
+    detours = n_inner == 2 and n_head == 2
+    partner = (seq, n_head - 1 - hd)
+    hop_device = (across[0], n_head - 1 - hd)
+    owes = jnp.logical_and(group == 0, hd == 1)
+    owed = jnp.logical_and(group == 0, hd == 0)
+    relays = jnp.logical_and(group == 1, hd == 0)
     barrier = pltpu.get_barrier_semaphore()
 
     def greet(p, carry):
@@ -148,6 +155,15 @@
         def _():
             pl.semaphore_wait(ready.at[0], 1)
 
+    if detours:
+        @pl.when(owed)
+        def _():
+            pl.semaphore_signal(ready.at[2], inc=1, device_id=partner, device_id_type=MESH)
+
+        @pl.when(owes)
+        def _():
+            pl.semaphore_wait(ready.at[2], 1)
+
     @pl.when(jnp.logical_not(last))
     def _():
         pl.semaphore_wait(ready.at[1], 1)
@@ -158,16 +174,27 @@
 
     def give(phase, c):
         def back(p, carry):
-            other, device = place(p)
+            other, device = place(jnp.where(group == 1, peers - p, p))
             for a in range(2):
-                pltpu.make_async_remote_copy(
-                    src_ref=xout.at[2 * phase + a, strip(other), cols(c)],
-                    dst_ref=targets[phase][a].at[:, column(me, c)],
-                    send_sem=out_send,
-                    recv_sem=out_recv,
-                    device_id=device,
-                    device_id_type=MESH,
-                ).start()
+                def send(dst, device, recv, a=a):
+                    pltpu.make_async_remote_copy(
+                        src_ref=xout.at[2 * phase + a, strip(other), cols(c)], dst_ref=dst,
+                        send_sem=out_send, recv_sem=recv, device_id=device, device_id_type=MESH,
+                    ).start()
+
+                target = targets[phase][a].at[:, column(me, c)]
+                if detours and phase == 0 and a < DETOUR_ARRAYS:
+                    detour = jnp.logical_and(owes, jnp.logical_and(c < DETOUR_CHUNKS, p == 1))
+
+                    @pl.when(detour)
+                    def _():
+                        send(hop.at[a, :, cols(c)], hop_device, hop_recv)
+
+                    @pl.when(jnp.logical_not(detour))
+                    def _():
+                        send(target, device, out_recv)
+                else:
+                    send(target, device, out_recv)
             return carry
 
         lax.fori_loop(1, peers, back, 0)
@@ -305,6 +332,17 @@
         return carry
 
     lax.fori_loop(0, 2 * chunks + 2 * n_outer, tick, 0)
+
+    if detours:
+        @pl.when(relays)
+        def _():
+            pltpu.make_async_copy(hop, hop, hop_recv).wait()
+            whole = pl.ds(pl.multiple_of((sub * heads + j * heads) * HEAD_DIM, span), hop.shape[2])
+            for a in range(DETOUR_ARRAYS):
+                pltpu.make_async_remote_copy(
+                    src_ref=hop.at[a], dst_ref=targets[0][a].at[:, whole], send_sem=hop_send,
+                    recv_sem=out_recv, device_id=across, device_id_type=MESH).start()
+            pltpu.make_async_copy(hop, hop, hop_send).wait()
 
     sent = xin.at[:, pl.ds(0, (peers - 1) * rows)]
     pltpu.make_async_copy(sent, sent, in_send).wait()
@@ -371,8 +409,9 @@
             pltpu.VMEM((heads, sub, HEAD_DIM, HEAD_DIM), BF16),
             state, state, state, state, state, state, state, state,
             pltpu.VMEM((local_heads * HEAD_DIM,), F32),
-            sems, chain, chain, chain, one, one, one, one, one, one, one, one,
-            pltpu.SemaphoreType.REGULAR((2,)),
+            pltpu.VMEM((DETOUR_ARRAYS, rows, DETOUR_CHUNKS * step * HEAD_DIM), BF16),
+            sems, chain, chain, chain, one, one, one, one, one, one, one, one, one, one,
+            pltpu.SemaphoreType.REGULAR((3,)),
         ],
         compiler_params=pltpu.CompilerParams(
             collective_id=0, has_side_effects=True, vmem_limit_bytes=51000 * 1024),

time: 97.5 us -> 97.2 us (level)
  no operation moved by 1% of the time
where the time goes in v4:
time: 97.2 us; the launch traced here: 96.8 us
  Pallas kernels  96.2 us (99%)
    pallas_call x1, Pallas kernels, per_device(): pl.pallas_call(functools.partial(kernel, plan), out_shape=shapes, in_spec...  94.2 us
    pallas_call x1, Pallas kernels, per_device(): pl.pallas_call(functools.partial(land, 4 if rows % 64 == 0 else 1), out_s...  2 us

profile of v4, /device:TPU:0, one launch (start us, length us, event | category | flops | bytes accessed | tf_op | source)
XLA Modules:
  0.0 96.8 jit_solution(5954283443617813699)
XLA Ops:
  0.6 94.2 %shard_map.93 = (bf16[64,8192]{1,0:T(8,128)(2,1)S(1)}, bf16[64,8192]{1,0:T(8,128)(2,1)S(1)}, bf16[64,8192]{1,0:T(8,128)(2,1)S(1)}, bf16[64,8192]{1,0:T(8,128)(2,1)S(1)}) custom-call(bf16[64,8192]{1,0:T(8,128)(2,1)} %q_hbm.1, bf16[64,8192]{1,0:T(8,128)(2,1)} %k_hbm.1, bf16[64,8192]{1,0:T(8,128)(2,1)} %v_hbm.1, bf16[64,8192]{1,0:T(8,128)(2,1)} %y_hbm.1, ...), custom_call_target="tpu_custom_call" | custom-call | tf_op jit(solution)/shard_map/pallas_call | solution.py:399
  94.8 2.0 %shard_map.94 = (bf16[64,8192]{1,0:T(8,128)(2,1)}, bf16[64,8192]{1,0:T(8,128)(2,1)}, bf16[64,8192]{1,0:T(8,128)(2,1)}, bf16[64,8192]{1,0:T(8,128)(2,1)}) custom-call(bf16[64,8192]{1,0:T(8,128)(2,1)S(1)} %get-tuple-element.8.refs_0_, bf16[64,8192]{1,0:T(8,128)(2,1)S(1)} %get-tuple-element.9.refs_1_, bf16[64,8192]{1,0:T(8,128)(2,1)S(1)} %get-tuple-element.10.refs_2_, ...), custom_call_target="tpu_custom_call" | custom-call | tf_op jit(solution)/shard_map/pallas_call | solution.py:420

commit v5 on v3

v5 whole, which is shorter than its diff:
```python
import functools

import jax
import jax.numpy as jnp
from jax import lax
from jax.experimental import pallas as pl
from jax.experimental.pallas import tpu as pltpu
from jax.sharding import PartitionSpec as P

HEAD_DIM = 128
EPSILON = 1e-06
DETOUR_ARRAYS, DETOUR_CHUNKS = 1, 1
MESH = pl.DeviceIdType.MESH
F32 = jnp.float32
BF16 = jnp.bfloat16

NT = (((1,), (1,)), ((), ()))
TN = (((0,), (0,)), ((), ()))
NN = (((1,), (0,)), ((), ()))


def dot(a, b, dims):
    return lax.dot_general(a, b, dims, preferred_element_type=F32)


def kernel(plan, q_hbm, k_hbm, v_hbm, y_hbm, gain_hbm, s0_hbm, o_out, gq_out, gk_out, gv_out,
           xin, xout, part, cum, gcum, prefix, tot, gtot, xt, xg, pin, psend, sin, ssend, gain, hop,
           first_recv, in_send, entered):
    n_outer, n_inner, sub, n_head, rows, heads, step = plan
    peers = sub * n_head
    chunks = heads // step
    block = rows * n_head
    span = step * HEAD_DIM
    seq, hd = lax.axis_index("seq"), lax.axis_index("head")
    group, j = seq // sub, lax.rem(seq, sub)
    outer, inner = group // n_inner, lax.rem(group, n_inner)
    me = j * n_head + hd

    def place(p):
        to_j = lax.rem(j + p // n_head, sub)
        to_hd = lax.rem(hd + lax.rem(p, n_head), n_head)
        return to_j * n_head + to_hd, (group * sub + to_j, to_hd)

    def column(other, c):
        owner = lax.rem(other, n_head) * (sub * heads) + (other // n_head) * heads + c * step
        return pl.ds(pl.multiple_of(owner * HEAD_DIM, span), span)

    def strip(index):
        return pl.ds(pl.multiple_of(index * rows, rows), rows)

    def cols(c):
        return pl.ds(pl.multiple_of(c * span, span), span)

    def piece(c):
        return pl.ds(c * step, step)

    across = ((outer * n_inner + (n_inner - 1 - inner)) * sub + j, hd)
    later = (seq + n_inner * sub, hd)
    earlier = (seq - n_inner * sub, hd)
    first, last = outer == 0, outer == n_outer - 1
    detours = n_inner == 2 and n_head == 2
    partner = (seq, n_head - 1 - hd)
    hop_device = (across[0], n_head - 1 - hd)
    owes = jnp.logical_and(group == 0, hd == 1)
    owed = jnp.logical_and(group == 0, hd == 0)
    relays = jnp.logical_and(group == 1, hd == 0)
    barrier = pltpu.get_barrier_semaphore()

    def greet(p, carry):
        _, device = place(p)
        pl.semaphore_signal(barrier, inc=1, device_id=device, device_id_type=MESH)
        return carry

    lax.fori_loop(1, peers, greet, 0)
    inside = inner == 0

    if n_inner == 2:
        @pl.when(inside)
        def _():
            pl.semaphore_signal(barrier, inc=1, device_id=across, device_id_type=MESH)

    @pl.when(jnp.logical_not(last))
    def _():
        pl.semaphore_signal(barrier, inc=1, device_id=later, device_id_type=MESH)

    sources = ((k_hbm, v_hbm), (q_hbm, y_hbm))
    targets = ((o_out, gq_out), (gk_out, gv_out))

    for more_x in range(n_inner):
        for more_z in range(2):
            @pl.when(jnp.logical_and(inner == more_x, first == (more_z == 0)))
            def _(more=more_x + more_z):
                pl.semaphore_wait(barrier, peers - 1 + more)

    def scatter(phase, recv):
        def chunk(c, carry):
            def one(p, carry):
                other, device = place(p)
                for a in range(2):
                    pltpu.make_async_remote_copy(
                        src_ref=sources[phase][a].at[:, column(other, c)],
                        dst_ref=xin.at[2 * phase + a, strip(me), cols(c)],
                        send_sem=in_send,
                        recv_sem=recv.at[c],
                        device_id=device,
                        device_id_type=MESH,
                    ).start()
                return carry

            lax.fori_loop(1, peers, one, 0)
            for a in range(2):
                pltpu.make_async_copy(
                    sources[phase][a].at[:, column(me, c)],
                    xin.at[2 * phase + a, strip(me), cols(c)],
                    recv.at[c],
                ).start()
            return carry

        lax.fori_loop(0, chunks, chunk, 0)

    scatter(0, first_recv)

    def rest(second_recv, chain_recv, t_recv, g_recv, out_send, out_recv,
             p_send, s_send, t_send, g_send, gain_sem, hop_send, hop_recv):
        in_recv = first_recv, second_recv

        def announce(p, carry):
            _, device = place(p)
            pl.semaphore_signal(entered.at[0], inc=1, device_id=device, device_id_type=MESH)
            return carry

        lax.fori_loop(1, peers, announce, 0)
        gains = pltpu.make_async_copy(gain_hbm, gain, gain_sem)
        gains.start()

        if n_inner == 2:
            @pl.when(jnp.logical_not(inside))
            def _():
                pl.semaphore_signal(entered.at[0], inc=1, device_id=across, device_id_type=MESH)

        @pl.when(jnp.logical_not(first))
        def _():
            pl.semaphore_signal(entered.at[0], inc=1, device_id=earlier, device_id_type=MESH)

        @pl.when(first)
        def _():
            def carried_in(c, carry):
                pltpu.make_async_copy(
                    s0_hbm.at[pl.ds(j * heads + c * step, step)], pin.at[piece(c)], chain_recv.at[c],
                ).start()
                return carry

            lax.fori_loop(0, chunks, carried_in, 0)

        @pl.when(last)
        def _():
            sin[...] = jnp.zeros_like(sin)

        row = lax.broadcasted_iota(jnp.int32, (block, block), 0)
        col = lax.broadcasted_iota(jnp.int32, (block, block), 1)
        causal = col <= row
        gains.wait()

        for more_x in range(n_inner):
            for more_z in range(2):
                @pl.when(jnp.logical_and(inner == n_inner - 1 - more_x, last == (more_z == 0)))
                def _(more=more_x + more_z):
                    pl.semaphore_wait(entered.at[0], peers - 1 + more)

        if n_inner == 2:
            @pl.when(inside)
            def _():
                pl.semaphore_signal(entered.at[1], inc=1, device_id=across, device_id_type=MESH)

        @pl.when(jnp.logical_not(last))
        def _():
            pl.semaphore_signal(entered.at[1], inc=1, device_id=later, device_id_type=MESH)

        if detours:
            @pl.when(owed)
            def _():
                pl.semaphore_signal(entered.at[2], inc=1, device_id=partner, device_id_type=MESH)

        scatter(1, second_recv)

        for more_x in range(n_inner):
            for more_z in range(2):
                if more_x + more_z > 0:
                    @pl.when(jnp.logical_and(inner == more_x, first == (more_z == 0)))
                    def _(more=more_x + more_z):
                        pl.semaphore_wait(entered.at[1], more)

        if detours:
            @pl.when(owes)
            def _():
                pl.semaphore_wait(entered.at[2], 1)

        def arrived(phase, c):
            ref = xin.at[pl.ds(2 * phase, 2), :, cols(c)]
            pltpu.make_async_copy(ref, ref, in_recv[phase].at[c]).wait()

        def give(phase, c):
            def back(p, carry):
                other, device = place(jnp.where(group == 1, peers - p, p))
                for a in range(2):
                    def send(dst, device, recv, a=a):
                        pltpu.make_async_remote_copy(
                            src_ref=xout.at[2 * phase + a, strip(other), cols(c)], dst_ref=dst,
                            send_sem=out_send, recv_sem=recv, device_id=device, device_id_type=MESH,
                        ).start()

                    target = targets[phase][a].at[:, column(me, c)]
                    if detours and phase == 0 and a < DETOUR_ARRAYS:
                        detour = jnp.logical_and(owes, jnp.logical_and(c < DETOUR_CHUNKS, p == 1))

                        @pl.when(detour)
                        def _():
                            send(hop.at[a, :, cols(c)], hop_device, hop_recv)

                        @pl.when(jnp.logical_not(detour))
                        def _():
                            send(target, device, out_recv)
                    else:
                        send(target, device, out_recv)
                return carry

            lax.fori_loop(1, peers, back, 0)
            for a in range(2):
                pltpu.make_async_copy(
                    xout.at[2 * phase + a, strip(me), cols(c)],
                    targets[phase][a].at[:, column(me, c)],
                    out_recv,
                ).start()

        def state_copy(src, dst, send, recv, c, device):
            return pltpu.make_async_remote_copy(
                src_ref=src.at[piece(c)], dst_ref=dst.at[piece(c)], send_sem=send,
                recv_sem=recv.at[c], device_id=device, device_id_type=MESH)

        def landed(ref, recv, c):
            pltpu.make_async_copy(ref.at[piece(c)], ref.at[piece(c)], recv.at[c]).wait()

        def lanes(c, h):
            return pl.ds(pl.multiple_of(c * span + h * HEAD_DIM, HEAD_DIM), HEAD_DIM)

        def block_states(c):
            arrived(0, c)
            for h in range(step):
                n, hc = c * step + h, lanes(c, h)
                run = dot(xin[0, :block, hc], xin[1, :block, hc], TN)
                for b in range(1, sub):
                    r = slice(b * block, (b + 1) * block)
                    cum[n, b - 1] = run
                    run = run + dot(xin[0, r, hc], xin[1, r, hc], TN)
                tot[n] = run
            if n_inner == 2:
                state_copy(tot, xt, t_send, t_recv, c, across).start()

        def pass_prefix(c):
            if n_inner == 2:
                landed(xt, t_recv, c)
            landed(pin, chain_recv, c)

            @pl.when(jnp.logical_not(last))
            def _():
                for h in range(step):
                    n = c * step + h
                    psend[n] = pin[n] + tot[n] + xt[n] if n_inner == 2 else pin[n] + tot[n]
                state_copy(psend, pin, p_send, chain_recv, c, later).start()

            for h in range(step):
                n = c * step + h
                before = pin[n]
                if n_inner == 2:
                    before = before + jnp.where(inner == 1, xt[n], 0.0)
                prefix[n, 0] = before.astype(BF16)
                for b in range(1, sub):
                    prefix[n, b] = (before + cum[n, b - 1]).astype(BF16)

        def attend(c):
            arrived(1, c)
            for h in range(step):
                n, hc = c * step + h, lanes(c, h)
                at = pl.multiple_of((j * heads + n) * HEAD_DIM, HEAD_DIM)
                g = gain[pl.ds(at, HEAD_DIM)].reshape(1, HEAD_DIM)
                run = None
                for b in reversed(range(sub)):
                    r = slice(b * block, (b + 1) * block)
                    k, v, q, up = xin[0, r, hc], xin[1, r, hc], xin[2, r, hc], xin[3, r, hc]
                    state = prefix[n, b]
                    w = jnp.where(causal, dot(q, k, NT), 0.0).astype(BF16)
                    att = dot(w, v, NN) + dot(q, state, NN)
                    inv = lax.rsqrt(jnp.mean(att * att, axis=-1, keepdims=True) + EPSILON)
                    normed = att * inv
                    xout[0, r, hc] = (normed * g).astype(BF16)
                    scaled = up.astype(F32) * g
                    ga = ((scaled - normed * jnp.mean(scaled * normed, axis=-1, keepdims=True))
                          * inv).astype(BF16)
                    gw = jnp.where(causal, dot(ga, v, NT), 0.0).astype(BF16)
                    xout[1, r, hc] = (dot(gw, k, NN) + dot(ga, state, NT)).astype(BF16)
                    part[0, r, hc] = dot(gw, q, TN)
                    part[1, r, hc] = dot(w, ga, TN)
                    if run is not None:
                        gcum[n, b] = run
                    grad = dot(q, ga, TN)
                    run = grad if run is None else run + grad
                gtot[n] = run
            if n_inner == 2:
                state_copy(gtot, xg, g_send, g_recv, c, across).start()
            give(0, c)

        def finish(c):
            if n_inner == 2:
                landed(xg, g_recv, c)

            @pl.when(jnp.logical_not(last))
            def _():
                landed(sin, chain_recv, c)

            @pl.when(jnp.logical_not(first))
            def _():
                for h in range(step):
                    n = c * step + h
                    ssend[n] = sin[n] + gtot[n] + xg[n] if n_inner == 2 else sin[n] + gtot[n]
                state_copy(ssend, sin, s_send, chain_recv, c, earlier).start()

            for h in range(step):
                n, hc = c * step + h, lanes(c, h)
                after = sin[n]
                if n_inner == 2:
                    after = after + jnp.where(inner == 0, xg[n], 0.0)
                for b in range(sub):
                    r = slice(b * block, (b + 1) * block)
                    suffix = (after + gcum[n, b] if b < sub - 1 else after).astype(BF16)
                    xout[2, r, hc] = (part[0, r, hc] + dot(xin[1, r, hc], suffix, NT)).astype(BF16)
                    xout[3, r, hc] = (part[1, r, hc] + dot(xin[0, r, hc], suffix, NN)).astype(BF16)
            give(1, c)

        prefix_lag = jnp.minimum(2 + 2 * outer, chunks)
        suffix_lag = chunks + 2 + 2 * (n_outer - 1 - outer)

        def tick(i, carry):
            @pl.when(i < chunks)
            def _():
                block_states(i)

            @pl.when(jnp.logical_and(i >= prefix_lag, i < prefix_lag + chunks))
            def _():
                pass_prefix(i - prefix_lag)

            @pl.when(jnp.logical_and(i >= chunks, i < 2 * chunks))
            def _():
                attend(i - chunks)

            @pl.when(jnp.logical_and(i >= suffix_lag, i < suffix_lag + chunks))
            def _():
                finish(i - suffix_lag)

            return carry

        lax.fori_loop(0, 2 * chunks + 2 * n_outer, tick, 0)

        if detours:
            @pl.when(relays)
            def _():
                pltpu.make_async_copy(hop, hop, hop_recv).wait()
                whole = pl.ds(pl.multiple_of((sub * heads + j * heads) * HEAD_DIM, span), hop.shape[2])
                for a in range(DETOUR_ARRAYS):
                    pltpu.make_async_remote_copy(
                        src_ref=hop.at[a], dst_ref=targets[0][a].at[:, whole], send_sem=hop_send,
                        recv_sem=out_recv, device_id=across, device_id_type=MESH).start()
                pltpu.make_async_copy(hop, hop, hop_send).wait()

        sent = xin.at[:, pl.ds(0, (peers - 1) * rows)]
        pltpu.make_async_copy(sent, sent, in_send).wait()
        pltpu.make_async_copy(sent, sent, out_send).wait()
        if n_inner == 2:
            pltpu.make_async_copy(tot, tot, t_send).wait()
            pltpu.make_async_copy(gtot, gtot, g_send).wait()

        @pl.when(jnp.logical_not(last))
        def _():
            pltpu.make_async_copy(psend, psend, p_send).wait()

        @pl.when(jnp.logical_not(first))
        def _():
            pltpu.make_async_copy(ssend, ssend, s_send).wait()

        pltpu.make_async_copy(xout, xout, out_recv).wait()

    one = pltpu.SemaphoreType.DMA
    chain = one((chunks,))
    pl.run_scoped(rest, chain, chain, chain, chain, *[one] * 9)


def land(parts, *refs):
    sources, targets, sem = refs[:4], refs[4:8], refs[8]
    copies = []
    rows = sources[0].shape[0] // parts
    for part in range(parts):
        for src, dst in zip(sources, targets):
            piece = pl.ds(part * rows, rows)
            copies.append(pltpu.make_async_copy(src.at[piece], dst.at[piece], sem))
            copies[-1].start()
    for copy in copies:
        copy.wait()


def per_device(mesh, query, key, value, cotangent, gain, incoming_state):
    n_seq, n_head = mesh.shape["seq"], mesh.shape["head"]
    rows, features = query.shape
    local_heads = incoming_state.shape[0]
    sub = 2 if n_seq % 2 == 0 and local_heads % 2 == 0 else 1
    n_inner = 2 if n_seq % (2 * sub) == 0 else 1
    n_outer = n_seq // (sub * n_inner)
    heads = local_heads // sub
    step = next(s for s in range(max(1, heads // 8), heads + 1) if heads % s == 0)
    chunks = heads // step
    tokens = rows * n_head * sub
    width = heads * HEAD_DIM
    plan = (n_outer, n_inner, sub, n_head, rows, heads, step)
    anywhere = pl.BlockSpec(memory_space=pl.ANY)
    resident = pl.BlockSpec(memory_space=pltpu.HBM)
    state = pltpu.VMEM((heads, HEAD_DIM, HEAD_DIM), F32)
    states = pltpu.VMEM((heads, max(1, sub - 1), HEAD_DIM, HEAD_DIM), F32)
    shapes = [jax.ShapeDtypeStruct((rows, features), BF16)] * 4
    results = pl.pallas_call(
        functools.partial(kernel, plan),
        out_shape=shapes,
        in_specs=[resident] * 6,
        out_specs=[anywhere] * 4,
        scratch_shapes=[
            pltpu.VMEM((4, tokens, width), BF16),
            pltpu.VMEM((4, tokens, width), BF16),
            pltpu.VMEM((2, tokens, width), F32),
            states, states,
            pltpu.VMEM((heads, sub, HEAD_DIM, HEAD_DIM), BF16),
            state, state, state, state, state, state, state, state,
            pltpu.VMEM((local_heads * HEAD_DIM,), F32),
            pltpu.VMEM((DETOUR_ARRAYS, rows, DETOUR_CHUNKS * step * HEAD_DIM), BF16),
            pltpu.SemaphoreType.DMA((chunks,)), pltpu.SemaphoreType.DMA,
            pltpu.SemaphoreType.REGULAR((3,)),
        ],
        compiler_params=pltpu.CompilerParams(
            collective_id=0, has_side_effects=True, vmem_limit_bytes=51000 * 1024),
    )(query, key, value, cotangent, pltpu.with_memory_space_constraint(gain, pltpu.HBM),
      incoming_state)
    return pl.pallas_call(
        functools.partial(land, 4 if rows % 64 == 0 else 1),
        out_shape=shapes,
        in_specs=[anywhere] * 4,
        out_specs=[anywhere] * 4,
        scratch_shapes=[pltpu.SemaphoreType.DMA],
        compiler_params=pltpu.CompilerParams(vmem_limit_bytes=1024 * 1024),
    )(*results)


def solution(mesh):
    tokens = P(("seq", "head"), None)
    return jax.shard_map(
        functools.partial(per_device, mesh),
        mesh=mesh,
        in_specs=(tokens, tokens, tokens, tokens, P("head"), P("head", None, None)),
        out_specs=(tokens, tokens, tokens, tokens),
        check_vma=False,
    )
```

time: 97.5 us -> 96.8 us (level)
  no operation moved by 1% of the time
where the time goes in v5:
time: 96.8 us; the launch traced here: 96.5 us
  Pallas kernels  95.8 us (99%)
    pallas_call x1, Pallas kernels, per_device(): pl.pallas_call(functools.partial(kernel, plan), out_shape=shapes, in_spec...  93.8 us
    pallas_call x1, Pallas kernels, per_device(): pl.pallas_call(functools.partial(land, 4 if rows % 64 == 0 else 1), out_s...  2 us

profile of v5, /device:TPU:0, one launch (start us, length us, event | category | flops | bytes accessed | tf_op | source)
XLA Modules:
  0.0 96.5 jit_solution(12207731655205026847)
XLA Ops:
  0.6 93.8 %shard_map.93 = (bf16[64,8192]{1,0:T(8,128)(2,1)S(1)}, bf16[64,8192]{1,0:T(8,128)(2,1)S(1)}, bf16[64,8192]{1,0:T(8,128)(2,1)S(1)}, bf16[64,8192]{1,0:T(8,128)(2,1)S(1)}) custom-call(bf16[64,8192]{1,0:T(8,128)(2,1)} %q_hbm.1, bf16[64,8192]{1,0:T(8,128)(2,1)} %k_hbm.1, bf16[64,8192]{1,0:T(8,128)(2,1)} %v_hbm.1, bf16[64,8192]{1,0:T(8,128)(2,1)} %y_hbm.1, ...), custom_call_target="tpu_custom_call" | custom-call | tf_op jit(solution)/shard_map/pallas_call | solution.py:427
  94.5 2.0 %shard_map.94 = (bf16[64,8192]{1,0:T(8,128)(2,1)}, bf16[64,8192]{1,0:T(8,128)(2,1)}, bf16[64,8192]{1,0:T(8,128)(2,1)}, bf16[64,8192]{1,0:T(8,128)(2,1)}) custom-call(bf16[64,8192]{1,0:T(8,128)(2,1)S(1)} %get-tuple-element.8.refs_0_, bf16[64,8192]{1,0:T(8,128)(2,1)S(1)} %get-tuple-element.9.refs_1_, bf16[64,8192]{1,0:T(8,128)(2,1)S(1)} %get-tuple-element.10.refs_2_, ...), custom_call_target="tpu_custom_call" | custom-call | tf_op jit(solution)/shard_map/pallas_call | solution.py:448

commit v6 on v5

--- a/solution.py
+++ b/solution.py
@@ -58,12 +58,14 @@
     later = (seq + n_inner * sub, hd)
     earlier = (seq - n_inner * sub, hd)
     first, last = outer == 0, outer == n_outer - 1
-    detours = n_inner == 2 and n_head == 2
+    detours = n_outer > 1 and n_inner == 2 and n_head == 2
     partner = (seq, n_head - 1 - hd)
-    hop_device = (across[0], n_head - 1 - hd)
+    by_x = j == 0
+    hop_device = (jnp.where(by_x, across[0], later[0]), n_head - 1 - hd)
     owes = jnp.logical_and(group == 0, hd == 1)
     owed = jnp.logical_and(group == 0, hd == 0)
-    relays = jnp.logical_and(group == 1, hd == 0)
+    relays = jnp.logical_and(group == jnp.where(by_x, 1, n_inner), hd == 0)
+    passed_to = (jnp.where(by_x, across[0], earlier[0]), hd)
     barrier = pltpu.get_barrier_semaphore()
 
     def greet(p, carry):
@@ -201,7 +203,7 @@
 
         def give(phase, c):
             def back(p, carry):
-                other, device = place(jnp.where(group == 1, peers - p, p))
+                other, device = place(p)
                 for a in range(2):
                     def send(dst, device, recv, a=a):
                         pltpu.make_async_remote_copy(
@@ -368,7 +370,7 @@
                 for a in range(DETOUR_ARRAYS):
                     pltpu.make_async_remote_copy(
                         src_ref=hop.at[a], dst_ref=targets[0][a].at[:, whole], send_sem=hop_send,
-                        recv_sem=out_recv, device_id=across, device_id_type=MESH).start()
+                        recv_sem=out_recv, device_id=passed_to, device_id_type=MESH).start()
                 pltpu.make_async_copy(hop, hop, hop_send).wait()
 
         sent = xin.at[:, pl.ds(0, (peers - 1) * rows)]

time: 96.8 us -> 96.6 us (level)
  no operation moved by 1% of the time
where the time goes in v6:
time: 96.6 us; the launch traced here: 96.5 us
  Pallas kernels  95.8 us (99%)
    pallas_call x1, Pallas kernels, per_device(): pl.pallas_call(functools.partial(kernel, plan), out_shape=shapes, in_spec...  93.8 us
    pallas_call x1, Pallas kernels, per_device(): pl.pallas_call(functools.partial(land, 4 if rows % 64 == 0 else 1), out_s...  2 us

profile of v6, /device:TPU:0, one launch (start us, length us, event | category | flops | bytes accessed | tf_op | source)
XLA Modules:
  0.0 96.5 jit_solution(5608609169636049403)
XLA Ops:
  0.6 93.8 %shard_map.93 = (bf16[64,8192]{1,0:T(8,128)(2,1)S(1)}, bf16[64,8192]{1,0:T(8,128)(2,1)S(1)}, bf16[64,8192]{1,0:T(8,128)(2,1)S(1)}, bf16[64,8192]{1,0:T(8,128)(2,1)S(1)}) custom-call(bf16[64,8192]{1,0:T(8,128)(2,1)} %q_hbm.1, bf16[64,8192]{1,0:T(8,128)(2,1)} %k_hbm.1, bf16[64,8192]{1,0:T(8,128)(2,1)} %v_hbm.1, bf16[64,8192]{1,0:T(8,128)(2,1)} %y_hbm.1, ...), custom_call_target="tpu_custom_call" | custom-call | tf_op jit(solution)/shard_map/pallas_call | solution.py:429
  94.5 2.0 %shard_map.94 = (bf16[64,8192]{1,0:T(8,128)(2,1)}, bf16[64,8192]{1,0:T(8,128)(2,1)}, bf16[64,8192]{1,0:T(8,128)(2,1)}, bf16[64,8192]{1,0:T(8,128)(2,1)}) custom-call(bf16[64,8192]{1,0:T(8,128)(2,1)S(1)} %get-tuple-element.8.refs_0_, bf16[64,8192]{1,0:T(8,128)(2,1)S(1)} %get-tuple-element.9.refs_1_, bf16[64,8192]{1,0:T(8,128)(2,1)S(1)} %get-tuple-element.10.refs_2_, ...), custom_call_target="tpu_custom_call" | custom-call | tf_op jit(solution)/shard_map/pallas_call | solution.py:450

commit v7 on v6

--- a/solution.py
+++ b/solution.py
@@ -9,6 +9,7 @@
 
 HEAD_DIM = 128
 EPSILON = 1e-06
+VMEM = 36000 * 1024
 DETOUR_ARRAYS, DETOUR_CHUNKS = 1, 1
 MESH = pl.DeviceIdType.MESH
 F32 = jnp.float32
@@ -24,9 +25,9 @@
 
 
 def kernel(plan, q_hbm, k_hbm, v_hbm, y_hbm, gain_hbm, s0_hbm, o_out, gq_out, gk_out, gv_out,
-           xin, xout, part, cum, gcum, prefix, tot, gtot, xt, xg, pin, psend, sin, ssend, gain, hop,
+           hold, tail, xin, xout, part, cum, gcum, prefix, tot, gtot, xt, xg, pin, psend, sin, ssend, gain, hop,
            first_recv, in_send, entered):
-    n_outer, n_inner, sub, n_head, rows, heads, step = plan
+    n_outer, n_inner, sub, n_head, rows, heads, step, late = plan
     peers = sub * n_head
     chunks = heads // step
     block = rows * n_head
@@ -123,7 +124,8 @@
     scatter(0, first_recv)
 
     def rest(second_recv, chain_recv, t_recv, g_recv, out_send, out_recv,
-             p_send, s_send, t_send, g_send, gain_sem, hop_send, hop_recv):
+             p_send, s_send, t_send, g_send, gain_sem, hop_send, hop_recv, own_sem, hold_sem,
+             tail_send, tail_recv):
         in_recv = first_recv, second_recv
 
         def announce(p, carry):
@@ -222,6 +224,19 @@
                         @pl.when(jnp.logical_not(detour))
                         def _():
                             send(target, device, out_recv)
+                    elif late and phase == 1:
+                        held = jnp.logical_and(p == 1, c >= chunks - late)
+
+                        @pl.when(held)
+                        def _(a=a):
+                            at = pl.multiple_of((c - (chunks - late)) * span, span)
+                            pltpu.make_async_copy(
+                                xout.at[2 + a, strip(other), cols(c)],
+                                hold.at[a, :, pl.ds(at, span)], hold_sem).start()
+
+                        @pl.when(jnp.logical_not(held))
+                        def _():
+                            send(target, device, out_recv)
                     else:
                         send(target, device, out_recv)
                 return carry
@@ -231,7 +246,7 @@
                 pltpu.make_async_copy(
                     xout.at[2 * phase + a, strip(me), cols(c)],
                     targets[phase][a].at[:, column(me, c)],
-                    out_recv,
+                    own_sem,
                 ).start()
 
         def state_copy(src, dst, send, recv, c, device):
@@ -374,8 +389,21 @@
                 pltpu.make_async_copy(hop, hop, hop_send).wait()
 
         sent = xin.at[:, pl.ds(0, (peers - 1) * rows)]
+        back = xin.at[:, :, pl.ds(0, 5 * chunks // 8 * span)] if late else sent
+        mine = xin.at[:, pl.ds(0, rows)]
+        if late:
+            to_partner = pltpu.make_async_remote_copy(
+                src_ref=hold, dst_ref=tail, send_sem=tail_send, recv_sem=tail_recv,
+                device_id=partner, device_id_type=MESH)
+            pltpu.make_async_copy(hold, hold, hold_sem).wait()
+
+            @pl.when(j == sub - 1)
+            def _():
+                to_partner.start()
+
         pltpu.make_async_copy(sent, sent, in_send).wait()
-        pltpu.make_async_copy(sent, sent, out_send).wait()
+        pltpu.make_async_copy(back, back, out_send).wait()
+        pltpu.make_async_copy(mine, mine, own_sem).wait()
         if n_inner == 2:
             pltpu.make_async_copy(tot, tot, t_send).wait()
             pltpu.make_async_copy(gtot, gtot, g_send).wait()
@@ -388,22 +416,57 @@
         def _():
             pltpu.make_async_copy(ssend, ssend, s_send).wait()
 
-        pltpu.make_async_copy(xout, xout, out_recv).wait()
+        pltpu.make_async_copy(back, back, out_recv).wait()
+        if late:
+            @pl.when(j == sub - 1)
+            def _():
+                to_partner.wait()
 
     one = pltpu.SemaphoreType.DMA
     chain = one((chunks,))
-    pl.run_scoped(rest, chain, chain, chain, chain, *[one] * 9)
-
-
-def land(parts, *refs):
-    sources, targets, sem = refs[:4], refs[4:8], refs[8]
-    copies = []
-    rows = sources[0].shape[0] // parts
-    for part in range(parts):
-        for src, dst in zip(sources, targets):
-            piece = pl.ds(part * rows, rows)
-            copies.append(pltpu.make_async_copy(src.at[piece], dst.at[piece], sem))
-            copies[-1].start()
+    pl.run_scoped(rest, chain, chain, chain, chain, *[one] * 13)
+
+
+def land(*refs):
+    sources, targets, sem = refs[:4], refs[-5:-1], refs[-1]
+    copies = [pltpu.make_async_copy(src, dst, sem) for src, dst in zip(sources, targets)]
+    for copy in copies:
+        copy.start()
+    for copy in copies:
+        copy.wait()
+
+
+def last_pieces(sub, hold, tail, written, out, sem, send, recv):
+    seq, hd = lax.axis_index("seq"), lax.axis_index("head")
+    partner = (seq, 1 - hd)
+    barrier = pltpu.get_barrier_semaphore()
+
+    @pl.when(lax.rem(seq, sub) < sub - 1)
+    def _():
+        pl.semaphore_signal(barrier, inc=1, device_id=partner, device_id_type=MESH)
+        pl.semaphore_wait(barrier, 1)
+        copy = pltpu.make_async_remote_copy(
+            src_ref=hold, dst_ref=out, send_sem=send, recv_sem=recv,
+            device_id=partner, device_id_type=MESH)
+        copy.start()
+        copy.wait()
+
+    @pl.when(lax.rem(seq, sub) == sub - 1)
+    def _():
+        copy = pltpu.make_async_copy(tail, out, sem)
+        copy.start()
+        copy.wait()
+
+
+def land_last(plan, tail, gk_in, gv_in, gk_out, gv_out, sem):
+    n_outer, n_inner, sub, n_head, rows, heads, step, late = plan
+    seq, hd = lax.axis_index("seq"), lax.axis_index("head")
+    first = (1 - hd) * (sub * heads) + lax.rem(seq, sub) * heads + heads - late * step
+    at = pl.ds(pl.multiple_of(first * HEAD_DIM, HEAD_DIM), late * step * HEAD_DIM)
+    copies = [pltpu.make_async_copy(tail.at[a], out.at[:, at], sem)
+              for a, out in enumerate((gk_out, gv_out))]
+    for copy in copies:
+        copy.start()
     for copy in copies:
         copy.wait()
 
@@ -420,17 +483,20 @@
     chunks = heads // step
     tokens = rows * n_head * sub
     width = heads * HEAD_DIM
-    plan = (n_outer, n_inner, sub, n_head, rows, heads, step)
+    splits = sub == 2 and n_head == 2 and n_inner == 2 and n_outer > 1 and chunks % 8 == 0
+    late = chunks if splits else 0
+    plan = (n_outer, n_inner, sub, n_head, rows, heads, step, late)
     anywhere = pl.BlockSpec(memory_space=pl.ANY)
     resident = pl.BlockSpec(memory_space=pltpu.HBM)
     state = pltpu.VMEM((heads, HEAD_DIM, HEAD_DIM), F32)
     states = pltpu.VMEM((heads, max(1, sub - 1), HEAD_DIM, HEAD_DIM), F32)
     shapes = [jax.ShapeDtypeStruct((rows, features), BF16)] * 4
-    results = pl.pallas_call(
+    pieces = [jax.ShapeDtypeStruct((2, rows, max(1, late) * step * HEAD_DIM), BF16)] * 2
+    *results, hold, tail = pl.pallas_call(
         functools.partial(kernel, plan),
-        out_shape=shapes,
+        out_shape=shapes + pieces,
         in_specs=[resident] * 6,
-        out_specs=[anywhere] * 4,
+        out_specs=[anywhere] * 6,
         scratch_shapes=[
             pltpu.VMEM((4, tokens, width), BF16),
             pltpu.VMEM((4, tokens, width), BF16),
@@ -444,17 +510,40 @@
             pltpu.SemaphoreType.REGULAR((3,)),
         ],
         compiler_params=pltpu.CompilerParams(
-            collective_id=0, has_side_effects=True, vmem_limit_bytes=51000 * 1024),
-    )(query, key, value, cotangent, pltpu.with_memory_space_constraint(gain, pltpu.HBM),
-      incoming_state)
-    return pl.pallas_call(
-        functools.partial(land, 4 if rows % 64 == 0 else 1),
+            collective_id=0, has_side_effects=True, vmem_limit_bytes=VMEM),
+    )(*(pltpu.with_memory_space_constraint(x, pltpu.HBM)
+        for x in (query, key, value, cotangent, gain, incoming_state)))
+    small = pltpu.CompilerParams(vmem_limit_bytes=1024 * 1024)
+    written = pl.pallas_call(
+        land,
         out_shape=shapes,
         in_specs=[anywhere] * 4,
         out_specs=[anywhere] * 4,
         scratch_shapes=[pltpu.SemaphoreType.DMA],
-        compiler_params=pltpu.CompilerParams(vmem_limit_bytes=1024 * 1024),
+        compiler_params=small,
     )(*results)
+    if not late:
+        return tuple(written)
+    output, grad_query, grad_key, grad_value = written
+    tail = pl.pallas_call(
+        functools.partial(last_pieces, sub),
+        out_shape=pieces[0],
+        in_specs=[anywhere] * 3,
+        out_specs=anywhere,
+        scratch_shapes=[pltpu.SemaphoreType.DMA] * 3,
+        compiler_params=pltpu.CompilerParams(
+            collective_id=1, has_side_effects=True, vmem_limit_bytes=1024 * 1024),
+    )(hold, tail, pltpu.with_memory_space_constraint(grad_key, pltpu.HBM))
+    grad_key, grad_value = pl.pallas_call(
+        functools.partial(land_last, plan),
+        out_shape=shapes[:2],
+        in_specs=[anywhere] * 3,
+        out_specs=[anywhere] * 2,
+        input_output_aliases={1: 0, 2: 1},
+        scratch_shapes=[pltpu.SemaphoreType.DMA],
+        compiler_params=small,
+    )(tail, grad_key, grad_value)
+    return output, grad_query, grad_key, grad_value
 
 
 def solution(mesh):

time: 96.6 us -> 96 us (level)
    pallas_call x2 -> x4, Pallas kernels: 95.8 us -> 95.2 us  [the longest x1 83.1 us: per_device(): pl.pallas_call(functools.partial(kernel, plan), out_shape=shapes + pieces...]
where the time goes in v7:
time: 96 us; the launch traced here: 95.8 us
  Pallas kernels  95.2 us (99%)
    pallas_call x1, Pallas kernels, per_device(): pl.pallas_call(functools.partial(kernel, plan), out_shape=shapes + pieces...  83.1 us
    pallas_call x1, Pallas kernels, per_device(): pl.pallas_call(functools.partial(last_pieces, sub), out_shape=pieces[0],...  9.24 us
    pallas_call x1, Pallas kernels, per_device(): pl.pallas_call(land, out_shape=shapes, in_specs=[anywhere] * 4, out_specs...  2.02 us

profile of v7, /device:TPU:0, one launch (start us, length us, event | category | flops | bytes accessed | tf_op | source)
XLA Modules:
  0.0 95.8 jit_solution(5252993863032478479)
XLA Ops:
  0.6 83.1 %shard_map.93 = (bf16[64,8192]{1,0:T(8,128)(2,1)S(1)}, bf16[64,8192]{1,0:T(8,128)(2,1)S(1)}, bf16[64,8192]{1,0:T(8,128)(2,1)S(1)}, bf16[64,8192]{1,0:T(8,128)(2,...) custom-call(bf16[64,8192]{1,0:T(8,128)(2,1)} %q_hbm.1, bf16[64,8192]{1,0:T(8,128)(2,1)} %k_hbm.1, ...), custom_call_target="tpu_custom_call" | custom-call | tf_op jit(solution)/shard_map/pallas_call | solution.py:495
  83.8 2.0 %shard_map.94 = (bf16[64,8192]{1,0:T(8,128)(2,1)}, bf16[64,8192]{1,0:T(8,128)(2,1)}, bf16[64,8192]{1,0:T(8,128)(2,1)}, bf16[64,8192]{1,0:T(8,128)(2,1)}) custom-call(bf16[64,8192]{1,0:T(8,128)(2,1)S(1)} %get-tuple-element.16.refs_0_, bf16[64,8192]{1,0:T(8,128)(2,1)S(1)} %get-tuple-element.17.refs_1_, bf16[64,8192]{1,0:T(8,128)(2,1)S(1)} %get-tuple-element.18.refs_2_, ...), custom_call_target="tpu_custom_call" | custom-call | tf_op jit(solution)/shard_map/pallas_call | solution.py:517
  85.8 9.2 %shard_map.95.tail = bf16[2,64,2048]{2,1,0:T(8,128)(2,1)S(1)} custom-call(bf16[2,64,2048]{2,1,0:T(8,128)(2,1)S(1)} %get-tuple-element.22.hold, bf16[2,64,2048]{2,1,0:T(8,128)(2,1)S(1)} %get-tuple-element.23.tail, bf16[64,8192]{1,0:T(8,128)(2,1)} %get-tuple-element.24.written.gk_in), custom_call_target="tpu_custom_call" | custom-call | tf_op jit(solution)/shard_map/pallas_call | solution.py:528
  95.0 0.8 shard_map.96

commit v8 on v7

--- a/solution.py
+++ b/solution.py
@@ -63,9 +63,8 @@
     partner = (seq, n_head - 1 - hd)
     by_x = j == 0
     hop_device = (jnp.where(by_x, across[0], later[0]), n_head - 1 - hd)
-    owes = jnp.logical_and(group == 0, hd == 1)
-    owed = jnp.logical_and(group == 0, hd == 0)
-    relays = jnp.logical_and(group == jnp.where(by_x, 1, n_inner), hd == 0)
+    owes = group == 0
+    relays = group == jnp.where(by_x, 1, n_inner)
     passed_to = (jnp.where(by_x, across[0], earlier[0]), hd)
     barrier = pltpu.get_barrier_semaphore()
 
@@ -181,7 +180,7 @@
             pl.semaphore_signal(entered.at[1], inc=1, device_id=later, device_id_type=MESH)
 
         if detours:
-            @pl.when(owed)
+            @pl.when(owes)
             def _():
                 pl.semaphore_signal(entered.at[2], inc=1, device_id=partner, device_id_type=MESH)
 
@@ -381,7 +380,8 @@
             @pl.when(relays)
             def _():
                 pltpu.make_async_copy(hop, hop, hop_recv).wait()
-                whole = pl.ds(pl.multiple_of((sub * heads + j * heads) * HEAD_DIM, span), hop.shape[2])
+                first_head = (1 - hd) * (sub * heads) + j * heads
+                whole = pl.ds(pl.multiple_of(first_head * HEAD_DIM, span), hop.shape[2])
                 for a in range(DETOUR_ARRAYS):
                     pltpu.make_async_remote_copy(
                         src_ref=hop.at[a], dst_ref=targets[0][a].at[:, whole], send_sem=hop_send,

time: 96 us -> 95.5 us (level)
  no operation moved by 1% of the time
where the time goes in v8:
time: 95.5 us; the launch traced here: 95.3 us
  Pallas kernels  94.7 us (99%)
    pallas_call x1, Pallas kernels, per_device(): pl.pallas_call(functools.partial(kernel, plan), out_shape=shapes + pieces...  82.4 us
    pallas_call x1, Pallas kernels, per_device(): pl.pallas_call(functools.partial(last_pieces, sub), out_shape=pieces[0],...  9.39 us
    pallas_call x1, Pallas kernels, per_device(): pl.pallas_call(land, out_shape=shapes, in_specs=[anywhere] * 4, out_specs...  2.02 us

profile of v8, /device:TPU:0, one launch (start us, length us, event | category | flops | bytes accessed | tf_op | source)
XLA Modules:
  0.0 95.3 jit_solution(11412294116816710223)
XLA Ops:
  0.6 82.4 %shard_map.93 = (bf16[64,8192]{1,0:T(8,128)(2,1)S(1)}, bf16[64,8192]{1,0:T(8,128)(2,1)S(1)}, bf16[64,8192]{1,0:T(8,128)(2,1)S(1)}, bf16[64,8192]{1,0:T(8,128)(2,...) custom-call(bf16[64,8192]{1,0:T(8,128)(2,1)} %q_hbm.1, bf16[64,8192]{1,0:T(8,128)(2,1)} %k_hbm.1, ...), custom_call_target="tpu_custom_call" | custom-call | tf_op jit(solution)/shard_map/pallas_call | solution.py:495
  83.1 2.0 %shard_map.94 = (bf16[64,8192]{1,0:T(8,128)(2,1)}, bf16[64,8192]{1,0:T(8,128)(2,1)}, bf16[64,8192]{1,0:T(8,128)(2,1)}, bf16[64,8192]{1,0:T(8,128)(2,1)}) custom-call(bf16[64,8192]{1,0:T(8,128)(2,1)S(1)} %get-tuple-element.16.refs_0_, bf16[64,8192]{1,0:T(8,128)(2,1)S(1)} %get-tuple-element.17.refs_1_, bf16[64,8192]{1,0:T(8,128)(2,1)S(1)} %get-tuple-element.18.refs_2_, ...), custom_call_target="tpu_custom_call" | custom-call | tf_op jit(solution)/shard_map/pallas_call | solution.py:517
  85.1 9.4 %shard_map.95.tail = bf16[2,64,2048]{2,1,0:T(8,128)(2,1)S(1)} custom-call(bf16[2,64,2048]{2,1,0:T(8,128)(2,1)S(1)} %get-tuple-element.22.hold, bf16[2,64,2048]{2,1,0:T(8,128)(2,1)S(1)} %get-tuple-element.23.tail, bf16[64,8192]{1,0:T(8,128)(2,1)} %get-tuple-element.24.written.gk_in), custom_call_target="tpu_custom_call" | custom-call | tf_op jit(solution)/shard_map/pallas_call | solution.py:528
  94.5 0.8 shard_map.96

commit v9 on v8

--- a/solution.py
+++ b/solution.py
@@ -26,7 +26,7 @@
 
 def kernel(plan, q_hbm, k_hbm, v_hbm, y_hbm, gain_hbm, s0_hbm, o_out, gq_out, gk_out, gv_out,
            hold, tail, xin, xout, part, cum, gcum, prefix, tot, gtot, xt, xg, pin, psend, sin, ssend, gain, hop,
-           first_recv, in_send, entered):
+           stage, first_recv, in_send, stage_sem, entered):
     n_outer, n_inner, sub, n_head, rows, heads, step, late = plan
     peers = sub * n_head
     chunks = heads // step
@@ -88,13 +88,25 @@
     sources = ((k_hbm, v_hbm), (q_hbm, y_hbm))
     targets = ((o_out, gq_out), (gk_out, gv_out))
 
+    early = hd == 0
+    beside, beside_device = place(1)
+    staging = [
+        pltpu.make_async_copy(sources[0][a].at[:, column(beside, 0)], stage.at[a], stage_sem)
+        for a in range(2)
+    ]
+
+    @pl.when(early)
+    def _():
+        for copy in staging:
+            copy.start()
+
     for more_x in range(n_inner):
         for more_z in range(2):
             @pl.when(jnp.logical_and(inner == more_x, first == (more_z == 0)))
             def _(more=more_x + more_z):
                 pl.semaphore_wait(barrier, peers - 1 + more)
 
-    def scatter(phase, recv):
+    def scatter(phase, recv, staged):
         def chunk(c, carry):
             def one(p, carry):
                 other, device = place(p)
@@ -109,7 +121,7 @@
                     ).start()
                 return carry
 
-            lax.fori_loop(1, peers, one, 0)
+            lax.fori_loop(jnp.where(c < staged, 2, 1), peers, one, 0)
             for a in range(2):
                 pltpu.make_async_copy(
                     sources[phase][a].at[:, column(me, c)],
@@ -120,7 +132,20 @@
 
         lax.fori_loop(0, chunks, chunk, 0)
 
-    scatter(0, first_recv)
+    @pl.when(early)
+    def _():
+        pltpu.make_async_copy(stage, stage, stage_sem).wait()
+        for a in range(2):
+            pltpu.make_async_remote_copy(
+                src_ref=stage.at[a],
+                dst_ref=xin.at[a, strip(me), cols(0)],
+                send_sem=in_send,
+                recv_sem=first_recv.at[0],
+                device_id=beside_device,
+                device_id_type=MESH,
+            ).start()
+
+    scatter(0, first_recv, jnp.where(early, 1, 0))
 
     def rest(second_recv, chain_recv, t_recv, g_recv, out_send, out_recv,
              p_send, s_send, t_send, g_send, gain_sem, hop_send, hop_recv, own_sem, hold_sem,
@@ -184,7 +209,7 @@
             def _():
                 pl.semaphore_signal(entered.at[2], inc=1, device_id=partner, device_id_type=MESH)
 
-        scatter(1, second_recv)
+        scatter(1, second_recv, 0)
 
         for more_x in range(n_inner):
             for more_z in range(2):
@@ -506,7 +531,8 @@
             state, state, state, state, state, state, state, state,
             pltpu.VMEM((local_heads * HEAD_DIM,), F32),
             pltpu.VMEM((DETOUR_ARRAYS, rows, DETOUR_CHUNKS * step * HEAD_DIM), BF16),
-            pltpu.SemaphoreType.DMA((chunks,)), pltpu.SemaphoreType.DMA,
+            pltpu.VMEM((2, rows, step * HEAD_DIM), BF16),
+            pltpu.SemaphoreType.DMA((chunks,)), pltpu.SemaphoreType.DMA, pltpu.SemaphoreType.DMA,
             pltpu.SemaphoreType.REGULAR((3,)),
         ],
         compiler_params=pltpu.CompilerParams(

time: 95.5 us -> 95.5 us (level)
  no operation moved by 1% of the time
where the time goes in v9:
time: 95.5 us; the launch traced here: 95.3 us
  Pallas kernels  94.7 us (99%)
    pallas_call x1, Pallas kernels, per_device(): pl.pallas_call(functools.partial(kernel, plan), out_shape=shapes + pieces...  82.4 us
    pallas_call x1, Pallas kernels, per_device(): pl.pallas_call(functools.partial(last_pieces, sub), out_shape=pieces[0],...  9.42 us
    pallas_call x1, Pallas kernels, per_device(): pl.pallas_call(land, out_shape=shapes, in_specs=[anywhere] * 4, out_specs...  2.02 us

profile of v9, /device:TPU:0, one launch (start us, length us, event | category | flops | bytes accessed | tf_op | source)
XLA Modules:
  0.0 95.3 jit_solution(5927528688807898315)
XLA Ops:
  0.6 82.4 %shard_map.93 = (bf16[64,8192]{1,0:T(8,128)(2,1)S(1)}, bf16[64,8192]{1,0:T(8,128)(2,1)S(1)}, bf16[64,8192]{1,0:T(8,128)(2,1)S(1)}, bf16[64,8192]{1,0:T(8,128)(2,...) custom-call(bf16[64,8192]{1,0:T(8,128)(2,1)} %q_hbm.1, bf16[64,8192]{1,0:T(8,128)(2,1)} %k_hbm.1, ...), custom_call_target="tpu_custom_call" | custom-call | tf_op jit(solution)/shard_map/pallas_call | solution.py:520
  83.0 2.0 %shard_map.94 = (bf16[64,8192]{1,0:T(8,128)(2,1)}, bf16[64,8192]{1,0:T(8,128)(2,1)}, bf16[64,8192]{1,0:T(8,128)(2,1)}, bf16[64,8192]{1,0:T(8,128)(2,1)}) custom-call(bf16[64,8192]{1,0:T(8,128)(2,1)S(1)} %get-tuple-element.16.refs_0_, bf16[64,8192]{1,0:T(8,128)(2,1)S(1)} %get-tuple-element.17.refs_1_, bf16[64,8192]{1,0:T(8,128)(2,1)S(1)} %get-tuple-element.18.refs_2_, ...), custom_call_target="tpu_custom_call" | custom-call | tf_op jit(solution)/shard_map/pallas_call | solution.py:543
  85.1 9.4 %shard_map.95.tail = bf16[2,64,2048]{2,1,0:T(8,128)(2,1)S(1)} custom-call(bf16[2,64,2048]{2,1,0:T(8,128)(2,1)S(1)} %get-tuple-element.22.hold, bf16[2,64,2048]{2,1,0:T(8,128)(2,1)S(1)} %get-tuple-element.23.tail, bf16[64,8192]{1,0:T(8,128)(2,1)} %get-tuple-element.24.written.gk_in), custom_call_target="tpu_custom_call" | custom-call | tf_op jit(solution)/shard_map/pallas_call | solution.py:554
  94.5 0.8 shard_map.96

commit v10 on v9

--- a/solution.py
+++ b/solution.py
@@ -108,8 +108,8 @@
 
     def scatter(phase, recv, staged):
         def chunk(c, carry):
-            def one(p, carry):
-                other, device = place(p)
+            def one(q, carry):
+                other, device = place(jnp.where(q == 1, 1, peers + 1 - q))
                 for a in range(2):
                     pltpu.make_async_remote_copy(
                         src_ref=sources[phase][a].at[:, column(other, c)],

time: 95.5 us -> 95.5 us (level)
  no operation moved by 1% of the time
where the time goes in v10:
time: 95.5 us; the launch traced here: 95.3 us
  Pallas kernels  94.7 us (99%)
    pallas_call x1, Pallas kernels, per_device(): pl.pallas_call(functools.partial(kernel, plan), out_shape=shapes + pieces...  82.4 us
    pallas_call x1, Pallas kernels, per_device(): pl.pallas_call(functools.partial(last_pieces, sub), out_shape=pieces[0],...  9.42 us
    pallas_call x1, Pallas kernels, per_device(): pl.pallas_call(land, out_shape=shapes, in_specs=[anywhere] * 4, out_specs...  2.02 us

profile of v10, /device:TPU:0, one launch (start us, length us, event | category | flops | bytes accessed | tf_op | source)
XLA Modules:
  0.0 95.3 jit_solution(9616974533490699941)
XLA Ops:
  0.6 82.4 %shard_map.93 = (bf16[64,8192]{1,0:T(8,128)(2,1)S(1)}, bf16[64,8192]{1,0:T(8,128)(2,1)S(1)}, bf16[64,8192]{1,0:T(8,128)(2,1)S(1)}, bf16[64,8192]{1,0:T(8,128)(2,...) custom-call(bf16[64,8192]{1,0:T(8,128)(2,1)} %q_hbm.1, bf16[64,8192]{1,0:T(8,128)(2,1)} %k_hbm.1, ...), custom_call_target="tpu_custom_call" | custom-call | tf_op jit(solution)/shard_map/pallas_call | solution.py:520
  83.0 2.0 %shard_map.94 = (bf16[64,8192]{1,0:T(8,128)(2,1)}, bf16[64,8192]{1,0:T(8,128)(2,1)}, bf16[64,8192]{1,0:T(8,128)(2,1)}, bf16[64,8192]{1,0:T(8,128)(2,1)}) custom-call(bf16[64,8192]{1,0:T(8,128)(2,1)S(1)} %get-tuple-element.16.refs_0_, bf16[64,8192]{1,0:T(8,128)(2,1)S(1)} %get-tuple-element.17.refs_1_, bf16[64,8192]{1,0:T(8,128)(2,1)S(1)} %get-tuple-element.18.refs_2_, ...), custom_call_target="tpu_custom_call" | custom-call | tf_op jit(solution)/shard_map/pallas_call | solution.py:543
  85.1 9.4 %shard_map.95.tail = bf16[2,64,2048]{2,1,0:T(8,128)(2,1)S(1)} custom-call(bf16[2,64,2048]{2,1,0:T(8,128)(2,1)S(1)} %get-tuple-element.22.hold, bf16[2,64,2048]{2,1,0:T(8,128)(2,1)S(1)} %get-tuple-element.23.tail, bf16[64,8192]{1,0:T(8,128)(2,1)} %get-tuple-element.24.written.gk_in), custom_call_target="tpu_custom_call" | custom-call | tf_op jit(solution)/shard_map/pallas_call | solution.py:554
  94.5 0.8 shard_map.96
